TPU v7x, 256 devices: a whole 4x4x8 slice. The times are simulated.
256 devices in a mesh: replica: 4 (over y_hi, core), fsdp: 64 (over y_lo, x, z).
Axes of the slice: x: 4, y: 4 (y_hi: 2, y_lo: 2; y = y_hi * 2 + y_lo), z: 8, core: 2. Of those that a mesh axis runs over, the one named last changes fastest.
Arguments:
- layer_input: bfloat16 [2, 32768, 4096], P(None, ('replica', 'fsdp')), may hold values from -6 to 6
- queries: bfloat16 [2, 32768, 4096], P(None, ('replica', 'fsdp')), may hold values from -100 to 100
- keys: bfloat16 [2, 32768, 512], P(None, ('replica', 'fsdp')), may hold values from -8 to 8
- targets: bfloat16 [2, 32768, 4096], P(None, ('replica', 'fsdp')), may hold values from -6 to 6
- value_weight: float32 [4096, 512], P('fsdp'), may hold values from -6 to 6
- outer_momentum: float32 [4096, 512], P('fsdp'), may hold values from -0.6 to 0.6
Outputs:
- new_weight: float32 [4096, 512], P('fsdp')
- new_momentum: float32 [4096, 512], P('fsdp')
All inputs are finite; a program needn't handle non-finite values.
Results may differ from a plain program's by a relative error of at most 0.0017.
Values may be sent and summed in bfloat16 or wider, within the bound.
No kernel may reach another device: no remote copies, remote signals or barrier semaphores. Data moves between devices by JAX's collectives and lax.ppermute only.
A program may use at most 64 MiB of HBM per device.

v0:
```python
import math

import jax
import jax.numpy as jnp
from jax import lax
from jax.sharding import Mesh
from jax.sharding import PartitionSpec as P

D = 4096
QH = 32
KVH = 4
HD = 128
FSDP = ("fsdp_0", "fsdp_1", "fsdp_2")
REPLICA = ("replica_0", "replica_1")
REPLICA_FSDP = ("replica_0", "replica_1", "fsdp_0", "fsdp_1", "fsdp_2")


beta_one = 0.9
beta_two = 0.95
inner_rate = 0.05
decay_rate = 0.1
outer_rate = 0.7
outer_mu = 0.9


def sent_to_all(value, axis):
    size = lax.axis_size(axis)
    return lax.all_to_all(
        jnp.broadcast_to(value[None], (size, *value.shape)), axis, 0, 0, tiled=True
    )


def joined_along(parts, dim):
    shape = list(parts.shape[1:])
    shape[dim] *= parts.shape[0]
    return jnp.moveaxis(parts, 0, dim).reshape(shape)


def gather_directly(value, axis, dim):
    parts = sent_to_all(value, axis)
    return joined_along(parts, dim)


def whole_of(value, axes, dim):
    far, near = axes
    leading = sent_to_all(value, far)
    parts = jnp.swapaxes(sent_to_all(leading, near), 0, 1)
    return joined_along(parts.reshape(-1, *value.shape), dim)


def gather_in_order(value, axes, order):
    parts = value
    for k in order:
        parts = lax.all_gather(parts, axes[k])
    done = order[::-1]
    back = [done.index(k) for k in range(len(axes))]
    parts = parts.transpose(*back, *range(len(axes), parts.ndim))
    return parts.reshape(-1, *value.shape)


def gather_axes(value, axes, order, dim):
    return joined_along(gather_in_order(value, axes, order), dim)


def own_block(parts, axes, order):
    shape = [lax.axis_size(a) for a in axes]
    parts = parts.reshape(*shape, *parts.shape[1:])
    parts = parts.transpose(*order, *range(len(axes), parts.ndim))
    parts = parts.reshape(-1, *parts.shape[len(axes) :])
    for k in order:
        parts = lax.psum_scatter(parts, axes[k], scatter_dimension=0, tiled=True)
    return parts[0]


def split_up(value, dim, size):
    shape = value.shape
    parts = value.reshape(*shape[:dim], size, shape[dim] // size, *shape[dim + 1 :])
    return jnp.moveaxis(parts, dim, 0)


def scatter_axes(value, axes, order, dim):
    size = lax.axis_size(axes)
    return own_block(split_up(value, dim, size), axes, order)


def taken_together(value, axis):
    everything = sent_to_all(value, axis)
    return jnp.sum(everything, axis=0)


def shards(layer_input, queries, keys, targets, value_weight, outer_momentum):
    inner_steps = layer_input.shape[0]
    length = layer_input.shape[1]
    columns = value_weight.shape[1]
    shard_rows = value_weight.shape[0]
    fsdp_count = lax.axis_size(FSDP)
    replicas = lax.axis_size(REPLICA)
    tok_rep = length * fsdp_count
    group_size = QH // KVH
    adam_floor = math.sqrt(group_size / (tok_rep * D))
    causal = jnp.arange(length)[:, None] >= jnp.arange(length)[None, :]
    weights_now = value_weight
    moment_one = jnp.zeros_like(value_weight)
    moment_two = jnp.zeros_like(value_weight)
    for step_index in range(inner_steps):
        inputs = layer_input[step_index]
        shard_bf = weights_now.astype(jnp.bfloat16)
        fold_needed = True
        if step_index == 0:
            quarter_rows = shard_rows // replicas
            own_quarter = lax.dynamic_slice_in_dim(
                shard_bf, lax.axis_index(REPLICA) * quarter_rows, quarter_rows, 0
            )
            across = gather_directly(own_quarter[None], FSDP, 0)
            across = across.reshape(fsdp_count, 1, quarter_rows * columns)
            whole = whole_of(across, ("replica_0", "replica_1"), 1).reshape(
                fsdp_count * shard_rows, columns
            )
            product = jnp.dot(inputs, whole, preferred_element_type=jnp.float32)
            fold_needed = False
        if fold_needed:
            product = jnp.dot(
                inputs,
                gather_axes(shard_bf, FSDP, (0, 1, 2), 0),
                preferred_element_type=jnp.float32,
            )
        values = (product / math.sqrt(D)).astype(jnp.bfloat16)
        query_heads = queries[step_index].reshape(length, KVH, group_size, HD)
        key_heads = keys[step_index].reshape(length, KVH, HD)
        scores = jnp.einsum(
            "qgjd,kgd->gjqk", query_heads, key_heads, preferred_element_type=jnp.float32
        ) / math.sqrt(HD)
        scores = jnp.where(causal, scores, -1e30)
        highest = jnp.max(scores, axis=-1, keepdims=True)
        expd = jnp.exp(scores - highest)
        attention = (expd / jnp.sum(expd, axis=-1, keepdims=True)).astype(jnp.bfloat16)
        attended = jnp.einsum(
            "gjqk,kgd->qgjd",
            attention,
            values.reshape(length, KVH, HD),
            preferred_element_type=jnp.float32,
        ).reshape(length, QH * HD)
        out_grad = ((attended - targets[step_index].astype(jnp.float32)) / tok_rep).astype(
            jnp.bfloat16
        )
        value_grad = (
            jnp.einsum(
                "gjqk,qgjd->kgd",
                attention,
                out_grad.reshape(length, KVH, group_size, HD),
                preferred_element_type=jnp.float32,
            )
            .reshape(length, columns)
            .astype(jnp.bfloat16)
        )
        partial_grad = lax.dot_general(
            inputs, value_grad, (((0,), (0,)), ((), ())), preferred_element_type=jnp.float32
        )
        gradient = scatter_axes(partial_grad / math.sqrt(D), FSDP, (1, 2, 0), 0)
        moment_one = beta_one * moment_one + (1.0 - beta_one) * gradient
        moment_two = beta_two * moment_two + (1.0 - beta_two) * gradient * gradient
        corrected_one = moment_one / (1.0 - beta_one ** (step_index + 1))
        corrected_two = moment_two / (1.0 - beta_two ** (step_index + 1))
        weights_now = weights_now - inner_rate * (
            corrected_one / (jnp.sqrt(corrected_two) + adam_floor) + decay_rate * weights_now
        )
    total_delta = taken_together(value_weight - weights_now, REPLICA)
    mean_delta = total_delta / replicas
    new_momentum = outer_mu * outer_momentum + mean_delta
    new_weight = value_weight - outer_rate * (mean_delta + outer_mu * new_momentum)
    return (new_weight, new_momentum)


def solution(mesh):
    split = Mesh(
        mesh.devices.reshape(2, 2, 2, 4, 8),
        ("replica_0", "replica_1", "fsdp_0", "fsdp_1", "fsdp_2"),
    )
    in_specs = (
        P(None, REPLICA_FSDP, None),
        P(None, REPLICA_FSDP, None),
        P(None, REPLICA_FSDP, None),
        P(None, REPLICA_FSDP, None),
        P(FSDP, None),
        P(FSDP, None),
    )
    out_specs = (P(FSDP, None), P(FSDP, None))
    return jax.shard_map(
        shards, mesh=split, in_specs=in_specs, out_specs=out_specs, check_vma=False
    )
```

profile of v0, /device:TPU:1, one launch (start us, length us, event | category | flops | bytes accessed | tf_op | source)
XLA Modules:
  0.0 550.0 jit_solution(12244470125275403065)
XLA Ops:
  9.1 13.5 %all-to-all-start = ((bf16[64,1,16,512]{3,2,1,0:T(8,128)(2,1)}), bf16[64,1,16,512]{3,2,1,0:T(8,128)(2,1)S(1)}, u32[]{:S(2)}, u32[]{:S(2)}) async-start(bf16[64,1,16,512]{3,2,1,0:T(8,128)(2,1)} %broadcast_in_dim.44), calls=%async_computation | async-start | bytes 2097152 | tf_op jit(solution)/shard_map/all_to_all | solution.py:28
  30.0 20.6 %all-to-all-done = bf16[64,1,16,512]{3,2,1,0:T(8,128)(2,1)S(1)} async-done(((bf16[64,1,16,512]{3,2,1,0:T(8,128)(2,1)}), bf16[64,1,16,512]{3,2,1,0:T(8,128)(2,1)S(1)}, u32[]{:S(2)}, u32[]{:S(2)}) %all-to-all-start) | async-done | bytes 1048608 | tf_op jit(solution)/shard_map/all_to_all | solution.py:28
  52.7 4.8 all-to-all-start.1
  62.6 4.0 fusion.60
  66.6 15.0 %all-to-all-done.1 = bf16[2,64,1,8192]{3,1,2,0:T(8,128)(2,1)} async-done(((bf16[2,64,1,8192]{3,1,2,0:T(8,128)(2,1)}), bf16[2,64,1,8192]{3,1,2,0:T(8,128)(2,1)}, u32[]{:S(2)}, u32[]{:S(2)}) %all-to-all-start.1) | async-done | bytes 2097184 | tf_op jit(solution)/shard_map/all_to_all | solution.py:28
  83.6 10.2 %all_to_all.20 = bf16[2,2,64,1,8192]{4,2,1,3,0:T(8,128)(2,1)S(1)} all-to-all(bf16[2,2,64,1,8192]{4,2,1,3,0:T(8,128)(2,1)S(1)} %broadcast_in_dim.48), channel_id=1, replica_groups=mesh['replica_0'=2,'replica_1'=2,'fsdp_0'=2,'fsdp_1'=4,'fsdp_2'=8] {'rep..., dimensions={0} | all-to-all | bytes 8388608 | tf_op jit(solution)/shard_map/all_to_all | solution.py:28
  94.0 5.2 copy.71
  99.2 7.8 %reshape_reshape.12 = bf16[4096,512]{1,0:T(8,128)(2,1)} reshape(bf16[64,4,1,8192]{3,1,0,2:T(4,128)(2,1)} %copy.71) | data formatting | bytes 8388608 | tf_op jit(solution)/shard_map/reshape;reshape | solution.py:116
  114.4 5.7 %multiply_bitcast_fusion.1 = f32[4096,512]{0,1:T(8,128)} fusion(bf16[128,512]{0,1:T(8,128)(2,1)S(1)} %bitcast.179, bf16[2,128,4096]{2,1,0:T(8,128)(2,1)} %param.6), kind=kOutput, calls=%fused_computation.3 | convolution fusion | flops 538968064 | bytes 9568256 | tf_op jit(solution)/shard_map/dot_general | solution.py:156
  120.1 9.0 %copy.79 = f32[4096,512]{1,0:T(8,128)} copy(f32[4096,512]{0,1:T(8,128)} %multiply_bitcast_fusion.1) | data formatting | bytes 16777216 | tf_op jit(solution)/shard_map/div | solution.py:159
  129.1 8.4 %copy.80 = f32[4,8,2,64,512]{4,3,2,1,0:T(8,128)} copy(f32[4,8,2,64,512]{4,3,1,0,2:T(8,128)} %bitcast.166) | data formatting | bytes 16777216 | tf_op jit(solution)/shard_map/transpose | solution.py:68
  137.6 77.5 %reduce-scatter.7.cloned.1.call-done = f32[16,64,512]{2,1,0:T(8,128)} async-done(((f32[64,64,512]{2,1,0:T(8,128)}), f32[16,64,512]{2,1,0:T(8,128)}) %reduce-scatter.7.cloned.1.call-update) | async-done | bytes 2097168 | tf_op jit(solution)/shard_map/reduce_scatter | solution.py:71
  215.2 40.3 %reduce-scatter.9.cloned.1.call-done = f32[2,64,512]{2,1,0:T(8,128)} async-done(((f32[16,64,512]{2,1,0:T(8,128)}), f32[2,64,512]{2,1,0:T(8,128)}) %reduce-scatter.9.cloned.1.call-update) | async-done | bytes 262160 | tf_op jit(solution)/shard_map/reduce_scatter | solution.py:71
  255.5 22.2 %reduce-scatter.11.cloned.1.call-done = f32[1,64,512]{2,1,0:T(8,128)} async-done(((f32[2,64,512]{2,1,0:T(8,128)}), f32[1,64,512]{2,1,0:T(8,128)}) %reduce-scatter.11.cloned.1.call-update) | async-done | bytes 131088 | tf_op jit(solution)/shard_map/reduce_scatter | solution.py:71
  278.7 3.8 all-gather
  282.5 12.1 %all-gather.1 = bf16[8,64,512]{2,1,0:T(8,128)(2,1)} all-gather(bf16[2,64,512]{2,1,0:T(8,128)(2,1)S(1)} %bitcast.178), channel_id=3, replica_groups=mesh['replica_0'=2,'replica_1'=2,'fsdp_0'=2,'fsdp_1'=4,'fsdp_2'=8] {'fsd..., dimensions={0}, use_global_device_ids=true | all-gather | bytes 655360 | tf_op jit(solution)/shard_map/all_gather | solution.py:54
  299.7 53.6 %all-gather.5.cloned.1.call-done = bf16[32,2,64,512]{3,2,1,0:T(8,128)(2,1)} async-done(((bf16[4,2,64,512]{3,2,1,0:T(8,128)(2,1)}), bf16[32,2,64,512]{3,2,1,0:T(8,128)(2,1)}) %all-gather.5.cloned.1.call-update) | async-done | bytes 4194320 | tf_op jit(solution)/shard_map/all_gather | solution.py:54
  361.1 4.5 multiply_bitcast_fusion
  365.5 9.0 %copy.89 = f32[4096,512]{1,0:T(8,128)} copy(f32[4096,512]{0,1:T(8,128)} %multiply_bitcast_fusion) | data formatting | bytes 16777216 | tf_op jit(solution)/shard_map/div | solution.py:159
  374.6 8.4 %copy.90 = f32[4,8,2,64,512]{4,3,2,1,0:T(8,128)} copy(f32[4,8,2,64,512]{4,3,1,0,2:T(8,128)} %bitcast.167) | data formatting | bytes 16777216 | tf_op jit(solution)/shard_map/transpose | solution.py:68
  383.0 81.8 %reduce-scatter.13.cloned.1.call-done = f32[16,64,512]{2,1,0:T(8,128)} async-done(((f32[64,64,512]{2,1,0:T(8,128)}), f32[16,64,512]{2,1,0:T(8,128)}) %reduce-scatter.13.cloned.1.call-update) | async-done | bytes 2097168 | tf_op jit(solution)/shard_map/reduce_scatter | solution.py:71
  464.9 40.3 %reduce-scatter.15.cloned.1.call-done = f32[2,64,512]{2,1,0:T(8,128)} async-done(((f32[16,64,512]{2,1,0:T(8,128)}), f32[2,64,512]{2,1,0:T(8,128)}) %reduce-scatter.15.cloned.1.call-update) | async-done | bytes 262160 | tf_op jit(solution)/shard_map/reduce_scatter | solution.py:71
  505.2 22.2 %reduce-scatter.17.cloned.1.call-done = f32[1,64,512]{2,1,0:T(8,128)} async-done(((f32[2,64,512]{2,1,0:T(8,128)}), f32[1,64,512]{2,1,0:T(8,128)}) %reduce-scatter.17.cloned.1.call-update) | async-done | bytes 131088 | tf_op jit(solution)/shard_map/reduce_scatter | solution.py:71
  528.6 13.8 %all_to_all.21 = f32[4,64,512]{2,1,0:T(8,128)S(1)} all-to-all(f32[4,64,512]{2,1,0:T(8,128)S(1)} %broadcast_in_dim.51), channel_id=1, replica_groups=mesh['replica_0'=2,'replica_1'=2,'fsdp_0'=2,'fsdp_1'=4,'fsdp_2'=8] {'rep..., dimensions={0} | all-to-all | bytes 1048576 | tf_op jit(solution)/shard_map/all_to_all | solution.py:28
  (49 shorter events, 42.3 us)
Async XLA Ops:
  9.1 41.5 %all-to-all-start = ((bf16[64,1,16,512]{3,2,1,0:T(8,128)(2,1)}), bf16[64,1,16,512]{3,2,1,0:T(8,128)(2,1)S(1)}, u32[]{:S(2)}, u32[]{:S(2)}) async-start(bf16[64,1,16,512]{3,2,1,0:T(8,128)(2,1)} %broadcast_in_dim.44), calls=%async_computation | async-start | bytes 2097152 | tf_op jit(solution)/shard_map/all_to_all | solution.py:28
  52.7 28.8 %all-to-all-start.1 = ((bf16[2,64,1,8192]{3,1,2,0:T(8,128)(2,1)}), bf16[2,64,1,8192]{3,1,2,0:T(8,128)(2,1)}, u32[]{:S(2)}, u32[]{:S(2)}) async-start(bf16[2,64,1,8192]{3,1,2,0:T(8,128)(2,1)} %broadcast_in_dim.46), calls=%async_computation.1 | async-start | bytes 4194304 | tf_op jit(solution)/shard_map/all_to_all | solution.py:28
  57.5 157.5 %reduce-scatter.7.cloned.1.call-start = ((), (), s32[]{:S(2)}) async-start(), calls=%async_computation.10 | async-start | bytes 10485760 | tf_op jit(solution)/shard_map/reduce_scatter | solution.py:71
  137.5 140.2 %copy-start.1 = (f32[64,512]{1,0:T(8,128)S(1)}, f32[64,512]{1,0:T(8,128)}, u32[]{:S(2)}) copy-start(f32[64,512]{1,0:T(8,128)} %param.10) | copy-start | bytes 393220
  137.6 117.9 %reduce-scatter.9.cloned.1.call-start = ((), (), s32[]{:S(2)}) async-start(), calls=%async_computation.11 | async-start | bytes 2359296 | tf_op jit(solution)/shard_map/reduce_scatter | solution.py:71
  215.1 62.6 %reduce-scatter.11.cloned.1.call-start = ((), (), s32[]{:S(2)}) async-start(), calls=%async_computation.12 | async-start | bytes 393216 | tf_op jit(solution)/shard_map/reduce_scatter | solution.py:71
  255.5 97.8 %all-gather.5.cloned.1.call-start = ((), (), s32[]{:S(2)}) async-start(), calls=%async_computation.16 | async-start | bytes 4718592 | tf_op jit(solution)/shard_map/all_gather | solution.py:54
  294.6 170.2 %reduce-scatter.13.cloned.1.call-start = ((), (), s32[]{:S(2)}) async-start(), calls=%async_computation.13 | async-start | bytes 10485760 | tf_op jit(solution)/shard_map/reduce_scatter | solution.py:71
  353.3 2.9 copy-start
  383.0 144.5 %copy-start.2 = (f32[1,64,512]{2,1,0:T(8,128)S(1)}, f32[1,64,512]{2,1,0:T(8,128)}, u32[]{:S(2)}) copy-start(f32[1,64,512]{2,1,0:T(8,128)} %reduce-scatter.11.cloned.1.call-done) | copy-start | bytes 393220
  383.0 122.2 %reduce-scatter.15.cloned.1.call-start = ((), (), s32[]{:S(2)}) async-start(), calls=%async_computation.14 | async-start | bytes 2359296 | tf_op jit(solution)/shard_map/reduce_scatter | solution.py:71
  464.8 77.6 %copy-start.3 = (f32[64,512]{1,0:T(8,128)S(1)}, f32[64,512]{1,0:T(8,128)}, u32[]{:S(2)}) copy-start(f32[64,512]{1,0:T(8,128)} %param.11) | copy-start | bytes 393220
  464.9 62.6 %reduce-scatter.17.cloned.1.call-start = ((), (), s32[]{:S(2)}) async-start(), calls=%async_computation.15 | async-start | bytes 393216 | tf_op jit(solution)/shard_map/reduce_scatter | solution.py:71
Sparse Core Ops, SparseCore 0:
  137.7 77.3 reduce-scatter.6
  217.6 37.7 reduce-scatter.8
  257.9 19.7 reduce-scatter.10
  294.7 58.5 all-gather.4
  383.1 81.6 reduce-scatter.12
  467.4 37.7 reduce-scatter.14
  507.8 19.5 reduce-scatter.16
where the time goes:
time: 551 us; the launch traced here: 550 us
  waiting for transfers between devices  374 us (68%)
  local copies, waits for them, and re-layouts  68.7 us (12%)
  blocking collectives  39.8 us (7%)
  matrix products  28.6 us (5%)
  starting transfers between devices  18.8 us (3%)
  between operations  14.3 us (3%)
  other arithmetic  6.23 us (1%)
    reduce_scatter x6, waiting for transfers between devices, own_block(): parts = lax.psum_scatter(parts, axes[k], scatter_dimension=0, tiled=True)  284 us
    all_gather x1, waiting for transfers between devices, gather_in_order(): parts = lax.all_gather(parts, axes[k])  53.6 us
    all_to_all x2, waiting for transfers between devices, sent_to_all(): lax.all_to_all(jnp.broadcast_to(value[None], (size, *value.shape)), axis,...  35.6 us
    all_to_all x2, blocking collectives, sent_to_all(): lax.all_to_all(jnp.broadcast_to(value[None], (size, *value.shape)), axis,...  23.9 us
    all_to_all x2, starting transfers between devices, sent_to_all(): lax.all_to_all(jnp.broadcast_to(value[None], (size, *value.shape)), axis,...  18.3 us
    div x2, local copies, waits for them, and re-layouts, shards(): gradient = scatter_axes(partial_grad / math.sqrt(D), FSDP, (1, 2, 0), 0)  18 us
    transpose x2, local copies, waits for them, and re-layouts, own_block(): parts = parts.transpose(*order, *range(len(axes), parts.ndim))  16.8 us
    all_gather x2, blocking collectives, gather_in_order(): parts = lax.all_gather(parts, axes[k])  15.9 us
  transfers between devices with their start and end apart: 9, of which 9 were waited for; matrix products, arithmetic and copies ran while one was open for 4% of the time, Pallas kernels for 0%

commit v1 on v0

v1 whole, which is shorter than its diff:
```python
import math

import jax
import jax.numpy as jnp
from jax import lax
from jax.experimental import pallas as pl
from jax.experimental.pallas import tpu as pltpu
from jax.sharding import Mesh
from jax.sharding import PartitionSpec as P

D = 4096
QH = 32
KVH = 4
HD = 128
GROUP = QH // KVH
FSDP = ("y", "x", "z")
OWNERS = ("y", "z")
REPLICA = ("yh", "c")
ALL = ("yh", "c", "y", "x", "z")

beta_one = 0.9
beta_two = 0.95
inner_rate = 0.05
decay_rate = 0.1
outer_rate = 0.7
outer_mu = 0.9

F32 = jnp.float32
BF16 = jnp.bfloat16
PARAMS = pltpu.CompilerParams(vmem_limit_bytes=48 << 20)


def shape_of(shape, dtype):
    return jax.ShapeDtypeStruct(shape, dtype)


def attention_body(q_ref, k_ref, t_ref, out_ref, p_ref):
    length = k_ref.shape[0]
    keys = k_ref[...]
    row = lax.broadcasted_iota(jnp.int32, (length, length), 0)
    col = lax.broadcasted_iota(jnp.int32, (length, length), 1)
    causal = row >= col
    for j in range(GROUP):
        head = q_ref[:, j * HD : (j + 1) * HD]
        scores = lax.dot_general(head, keys, (((1,), (1,)), ((), ())), preferred_element_type=F32)
        scores = jnp.where(causal, scores / math.sqrt(HD), -1e30)
        expd = jnp.exp(scores - jnp.max(scores, axis=-1, keepdims=True))
        attention = expd / jnp.sum(expd, axis=-1, keepdims=True)
        rows = slice(j * length, (j + 1) * length)
        p_ref[rows, :length] = attention.astype(BF16)
        p_ref[rows, length:] = t_ref[:, j * HD : (j + 1) * HD]
    both = p_ref[...]
    out_ref[0, 0] = lax.dot_general(
        both[:, :length], both, (((0,), (0,)), ((), ())), preferred_element_type=F32
    )


def attention_sums(queries, keys, targets):
    steps, length = queries.shape[:2]
    wide = GROUP * HD
    return pl.pallas_call(
        attention_body,
        grid=(steps, KVH),
        in_specs=[
            pl.BlockSpec((pl.Squeezed(), length, wide), lambda s, g: (s, 0, g)),
            pl.BlockSpec((pl.Squeezed(), length, HD), lambda s, g: (s, 0, g)),
            pl.BlockSpec((pl.Squeezed(), length, wide), lambda s, g: (s, 0, g)),
        ],
        out_specs=pl.BlockSpec((1, 1, length, length + HD), lambda s, g: (s, g, 0, 0)),
        out_shape=shape_of((steps, KVH, length, length + HD), F32),
        scratch_shapes=[pltpu.VMEM((GROUP * length, length + HD), BF16)],
        compiler_params=PARAMS,
        name="attention_sums",
    )(queries, keys, targets)


def slab_body(place_ref, *refs):
    half = len(refs) // 2
    for k in range(half):
        refs[half + k][...] = refs[k][...]


def slabs_of(place, layer_input, step, ys, xs):
    _, length, width = layer_input.shape
    wide = width // (ys * xs)

    def source(k):
        return pl.BlockSpec(
            (pl.Squeezed(), length, wide),
            lambda y, place: (step, 0, y * xs + lax.rem(place[0] + k, xs)),
        )

    return pl.pallas_call(
        slab_body,
        grid_spec=pltpu.PrefetchScalarGridSpec(
            num_scalar_prefetch=1,
            grid=(ys,),
            in_specs=[source(k) for k in range(xs)],
            out_specs=[pl.BlockSpec((length, wide), lambda y, place: (0, y))] * xs,
        ),
        out_shape=[shape_of((length, ys * wide), BF16)] * xs,
        compiler_params=PARAMS,
        name="slabs",
    )(place, *[layer_input] * xs)


def values_body(*refs):
    xs = len(refs) // 2
    weights = refs[xs][...]
    for k in range(xs):
        part = jnp.dot(refs[k][...], weights, preferred_element_type=F32)
        out = refs[xs + 1 + k]
        out[...] = (part * (1.0 / math.sqrt(D))).astype(out.dtype)


def partial_values(slabs, gathered):
    shape = (slabs[0].shape[0], gathered.shape[-1])
    return pl.pallas_call(
        values_body,
        out_shape=[shape_of(shape, F32)] + [shape_of(shape, BF16)] * (len(slabs) - 1),
        compiler_params=PARAMS,
        name="partial_values",
    )(*slabs, gathered)


def value_grad_body(*refs, tok_rep, step):
    parts, sums, out_ref = refs[:-2], refs[-2], refs[-1]
    length = out_ref.shape[0]
    total = parts[0][...]
    for part in parts[1:]:
        total = total + part[...].astype(F32)
    values = total.astype(BF16)
    for h in range(KVH):
        m = sums[h, :, :length]
        n = sums[h, :, length:]
        high = m.astype(BF16)
        low = (m - high.astype(F32)).astype(BF16)
        cols = slice(h * HD, (h + 1) * HD)
        part = values[:, cols]
        attended = jnp.dot(high, part, preferred_element_type=F32) + jnp.dot(
            low, part, preferred_element_type=F32
        )
        out_ref[:, cols] = ((attended - n) * (1.0 / tok_rep)).astype(BF16)


def value_gradient(parts, sums, step, tok_rep):
    whole = pl.BlockSpec(parts[0].shape, lambda i: (0, 0))
    return pl.pallas_call(
        lambda *refs: value_grad_body(*refs, tok_rep=tok_rep, step=step),
        grid=(1,),
        in_specs=[whole] * len(parts)
        + [pl.BlockSpec((pl.Squeezed(), *sums.shape[1:]), lambda i: (step, 0, 0, 0))],
        out_specs=whole,
        out_shape=shape_of(parts[0].shape, BF16),
        compiler_params=PARAMS,
        name="value_gradient",
    )(*parts, sums)


def gradient_body(*refs):
    half = len(refs) // 2
    inputs = jnp.concatenate([r[...] for r in refs[:half]], axis=0)
    stacked = jnp.concatenate([r[...] for r in refs[half:-1]], axis=0)
    total = lax.dot_general(inputs, stacked, (((0,), (0,)), ((), ())), preferred_element_type=F32)
    refs[-1][...] = (total * (1.0 / math.sqrt(D))).astype(BF16)


def partial_gradient(slabs, grads):
    shape = (slabs[0].shape[1], grads[0].shape[-1])
    return pl.pallas_call(
        gradient_body,
        out_shape=shape_of(shape, BF16),
        compiler_params=PARAMS,
        name="partial_gradient",
    )(*slabs, *grads)


def adam_body(*refs, step, floor, last):
    if step == 0:
        recv, theta_ref, m_out, u_out, theta_out, sent = refs
    else:
        recv, theta_ref, m_ref, u_ref, start_ref, m_out, u_out, theta_out, sent = refs
    gradient = recv[0].astype(F32)
    for z in range(1, recv.shape[0]):
        gradient = gradient + recv[z].astype(F32)
    moment_one = (1.0 - beta_one) * gradient
    moment_two = (1.0 - beta_two) * gradient * gradient
    if step > 0:
        moment_one = beta_one * m_ref[...] + moment_one
        moment_two = beta_two * u_ref[...] + moment_two
    corrected_one = moment_one / (1.0 - beta_one ** (step + 1))
    corrected_two = moment_two / (1.0 - beta_two ** (step + 1))
    theta = theta_ref[...]
    theta = theta - inner_rate * (
        corrected_one / (jnp.sqrt(corrected_two) + floor) + decay_rate * theta
    )
    m_out[...] = moment_one
    u_out[...] = moment_two
    theta_out[...] = theta
    if last:
        sent[...] = start_ref[...] - theta
    else:
        rounded = theta.astype(BF16)
        for z in range(recv.shape[0]):
            sent[z] = rounded


def adam(received, state, step, floor, last):
    shape = received.shape[1:]
    sent = shape_of(shape, F32) if last else shape_of(received.shape, BF16)
    return pl.pallas_call(
        lambda *refs: adam_body(*refs, step=step, floor=floor, last=last),
        out_shape=[shape_of(shape, F32)] * 3 + [sent],
        compiler_params=PARAMS,
        name="adam",
    )(received, *state)


def shifted(value, axis, k):
    size = lax.axis_size(axis)
    return lax.ppermute(value, axis, [(i, (i + k) % size) for i in range(size)])


def flipped(value, axis, mask):
    size = lax.axis_size(axis)
    return lax.ppermute(value, axis, [(i, i ^ mask) for i in range(size)])


def shards(layer_input, queries, keys, targets, value_weight, outer_momentum):
    inner_steps, length, _ = layer_input.shape
    shard_rows, columns = value_weight.shape
    ys, xs, zs = (lax.axis_size(a) for a in FSDP)
    owners = ys * zs
    tok_rep = length * owners * xs
    replicas = lax.axis_size(REPLICA)
    floor = math.sqrt(GROUP / (tok_rep * D))
    place = lax.axis_index("x").astype(jnp.int32).reshape(1)

    def routed(source, step):
        slabs = slabs_of(place, source, step, ys, xs)
        return [slabs[0]] + [shifted(slabs[k], "x", k) for k in range(1, xs)]

    rounded = value_weight.astype(BF16)
    gathered = lax.all_to_all(
        jnp.broadcast_to(rounded[None], (owners, shard_rows, columns)), OWNERS, 0, 0, tiled=True
    )
    slabs = routed(layer_input, 0)
    sums = attention_sums(queries, keys, targets)

    theta = value_weight
    state = ()
    for step in range(inner_steps):
        last = step == inner_steps - 1
        weights = gathered.reshape(owners * shard_rows, columns)
        parts = partial_values(slabs, weights)
        parts = [parts[0]] + [shifted(parts[k], "x", -k) for k in range(1, xs)]
        grad = value_gradient(parts, sums, step, tok_rep)
        grads = [grad] + [shifted(grad, "x", k) for k in range(1, xs)]
        scattered = partial_gradient(slabs, grads)
        scattered = scattered.reshape(owners, shard_rows, columns)
        if not last:
            scattered, source = lax.optimization_barrier((scattered, layer_input))
            slabs = routed(source, step + 1)
        received = lax.all_to_all(scattered, OWNERS, 0, 0, tiled=True)
        if not last:
            received, slabs = lax.optimization_barrier((received, slabs))
        args = (theta,) if step == 0 else (theta, *state, value_weight)
        m, u, theta, sent = adam(received, args, step, floor, last)
        state = (m, u)
        if not last:
            gathered = lax.all_to_all(sent, OWNERS, 0, 0, tiled=True)

    chip = sent + flipped(sent, "c", 1)
    mean_delta = (chip + flipped(chip, "yh", 1)) / replicas
    new_momentum = outer_mu * outer_momentum + mean_delta
    new_weight = value_weight - outer_rate * (mean_delta + outer_mu * new_momentum)
    return (new_weight, new_momentum)


def solution(mesh):
    split = Mesh(mesh.devices.reshape(2, 2, 2, 4, 8), ALL)
    tokens = P(None, REPLICA + FSDP, None)
    in_specs = (tokens, tokens, tokens, tokens, P(FSDP, None), P(FSDP, None))
    out_specs = (P(FSDP, None), P(FSDP, None))
    return jax.shard_map(
        shards, mesh=split, in_specs=in_specs, out_specs=out_specs, check_vma=False
    )
```

time: 551 us -> 195 us (0.35)
  waiting for transfers between devices: 374 us -> 55.6 us
  local copies, waits for them, and re-layouts: 68.7 us -> 11.9 us
  matrix products: 28.6 us -> 0 us
  starting transfers between devices: 18.8 us -> 46.7 us
  blocking collectives: 39.8 us -> 63.4 us
  Pallas kernels: 0 us -> 14.2 us
  between operations: 14.3 us -> 0.85 us
    reduce_scatter x6 -> x0, waiting for transfers between devices: 284 us -> none  [own_block(): parts = lax.psum_scatter(parts, axes[k], scatter_dimension=0, tiled=True)]
    all_gather x1 -> x0, waiting for transfers between devices: 53.6 us -> none  [gather_in_order(): parts = lax.all_gather(parts, axes[k])]
    all_to_all x2, blocking collectives: 23.9 us -> 63.4 us  [the longest x1 33.3 us: shards(): received = lax.all_to_all(scattered, OWNERS, 0, 0, tiled=True)]
    ppermute x0 -> x20, waiting for transfers between devices: none -> 38.6 us  [the longest x18 33.9 us: shifted(): return lax.ppermute(value, axis, [(i, (i + k) % size) for i in range(size)])]
    ppermute x0 -> x20, starting transfers between devices: none -> 29.3 us  [the longest x18 23.7 us: shifted(): return lax.ppermute(value, axis, [(i, (i + k) % size) for i in range(size)])]
    transpose x4 -> x0, local copies, waits for them, and re-layouts: 24.8 us -> none  [the longest x2 16.8 us: own_block(): parts = parts.transpose(*order, *range(len(axes), parts.ndim))]
    dot_general x6 -> x0, matrix products: 22.5 us -> none  [the longest x2 10.1 us: shards(): lax.dot_general(inputs, value_grad, (((0,), (0,)), ((), ())), preferred_e...]
    all_to_all x2, waiting for transfers between devices: 35.6 us -> 17 us  [the longest x1 9.03 us: shards(): lax.all_to_all(jnp.broadcast_to(rounded[None], (owners, shard_rows, colum...]
  transfers between devices with their start and end apart: 9 -> 22, of which waited for: 9 -> 17; matrix products, arithmetic and copies ran while one was open for 4% -> 0% of each run, Pallas kernels for 0% -> 4%
where the time goes in v1:
time: 195 us; the launch traced here: 194 us
  blocking collectives  63.4 us (33%)
  waiting for transfers between devices  55.6 us (29%)
  starting transfers between devices  46.7 us (24%)
  Pallas kernels  14.2 us (7%)
  local copies, waits for them, and re-layouts  11.9 us (6%)
    ppermute x18, waiting for transfers between devices, shifted(): return lax.ppermute(value, axis, [(i, (i + k) % size) for i in range(size)])  33.9 us
    all_to_all x1, blocking collectives, shards(): received = lax.all_to_all(scattered, OWNERS, 0, 0, tiled=True)  33.3 us
    all_to_all x1, blocking collectives, shards(): gathered = lax.all_to_all(sent, OWNERS, 0, 0, tiled=True)  30.1 us
    ppermute x18, starting transfers between devices, shifted(): return lax.ppermute(value, axis, [(i, (i + k) % size) for i in range(size)])  23.7 us
    unnamed x44, local copies, waits for them, and re-layouts  10.8 us
    all_to_all x1, starting transfers between devices, shards(): lax.all_to_all(jnp.broadcast_to(rounded[None], (owners, shard_rows, colum...  10.1 us
    all_to_all x1, waiting for transfers between devices, shards(): lax.all_to_all(jnp.broadcast_to(rounded[None], (owners, shard_rows, colum...  9.03 us
    all_to_all x1, waiting for transfers between devices, shards(): received = lax.all_to_all(scattered, OWNERS, 0, 0, tiled=True)  8.01 us
  transfers between devices with their start and end apart: 22, of which 17 were waited for; matrix products, arithmetic and copies ran while one was open for 0% of the time, Pallas kernels for 4%

profile of v1, /device:TPU:1, one launch (start us, length us, event | category | flops | bytes accessed | tf_op | source)
XLA Modules:
  0.0 194.5 jit_solution(11055111378737753377)
XLA Ops:
  2.8 10.1 %all-to-all-start = ((bf16[16,64,512]{2,1,0:T(8,128)(2,1)}), bf16[16,64,512]{2,1,0:T(8,128)(2,1)S(1)}, u32[]{:S(2)}, u32[]{:S(2)}) async-start(bf16[16,64,512]{2,1,0:T(8,128)(2,1)} %broadcast_in_dim.2), calls=%async_computation | async-start | bytes 2097152 | tf_op jit(solution)/shard_map/all_to_all | solution.py:244
  14.7 2.5 %collective-permute-start.1 = (bf16[128,1024]{1,0:T(8,128)(2,1)S(1)}, bf16[128,1024]{1,0:T(8,128)(2,1)S(1)}, u32[]{:S(2)}, u32[]{:S(2)}) collective-permute-start(bf16[128,1024]{1,0:T(8,128)(2,1)S(1)} %get-tuple-element.32), channel_id=1, source_target_pairs={{0,16},{8,24},{16,0},{24,8},{1,17},{9,25},{17,1},{25,9},{2,18},{10... | collective-permute-start | bytes 786440 | tf_op jit(solution)/shard_map/ppermute | solution.py:221
  18.3 3.3 %collective-permute-done.refs_1_ = bf16[128,1024]{1,0:T(8,128)(2,1)S(1)} collective-permute-done((bf16[128,1024]{1,0:T(8,128)(2,1)S(1)}, bf16[128,1024]{1,0:T(8,128)(2,1)S(1)}, u32[]{:S(2)}, u32[]{:S(2)}) %collective-permute-start) | collective-permute-done | bytes 262176 | tf_op jit(solution)/shard_map/ppermute | solution.py:221
  22.3 5.9 %collective-permute-done.1.refs_2_ = bf16[128,1024]{1,0:T(8,128)(2,1)S(1)} collective-permute-done((bf16[128,1024]{1,0:T(8,128)(2,1)S(1)}, bf16[128,1024]{1,0:T(8,128)(2,1)S(1)}, u32[]{:S(2)}, u32[]{:S(2)}) %collective-permute-start.1) | collective-permute-done | bytes 262176 | tf_op jit(solution)/shard_map/ppermute | solution.py:221
  29.6 9.0 %all-to-all-done = bf16[16,64,512]{2,1,0:T(8,128)(2,1)S(1)} async-done(((bf16[16,64,512]{2,1,0:T(8,128)(2,1)}), bf16[16,64,512]{2,1,0:T(8,128)(2,1)S(1)}, u32[]{:S(2)}, u32[]{:S(2)}) %all-to-all-start) | async-done | bytes 1048608 | tf_op jit(solution)/shard_map/all_to_all | solution.py:244
  42.4 2.6 %collective-permute-start.3 = (bf16[128,512]{1,0:T(8,128)(2,1)S(1)}, bf16[128,512]{1,0:T(8,128)(2,1)S(1)}, u32[]{:S(2)}, u32[]{:S(2)}) collective-permute-start(bf16[128,512]{1,0:T(8,128)(2,1)S(1)} %get-tuple-element.35), channel_id=1, source_target_pairs={{0,24},{8,0},{16,8},{24,16},{1,25},{9,1},{17,9},{25,17},{2,26},{10... | collective-permute-start | bytes 393224 | tf_op jit(solution)/shard_map/ppermute | solution.py:221
  48.6 7.4 %attention_sums.1.refs_4_ = f32[2,4,128,256]{3,2,1,0:T(8,128)S(1)} custom-call(bf16[2,128,4096]{2,1,0:T(8,128)(2,1)S(1)} %copy-done.3, bf16[2,128,512]{2,1,0:T(8,128)(2,1)S(1)} %copy-done.20, bf16[2,128,4096]{2,1,0:T(8,128)(2,1)S(1)} %copy-done.4), custom_call_target="tpu_custom_call" | custom-call | tf_op jit(solution)/shard_map/attention_sums/pallas_call | solution.py:61
  56.3 2.1 %collective-permute-start.8 = (bf16[128,512]{1,0:T(8,128)(2,1)S(1)}, bf16[128,512]{1,0:T(8,128)(2,1)S(1)}, u32[]{:S(2)}, u32[]{:S(2)}) collective-permute-start(bf16[128,512]{1,0:T(8,128)(2,1)S(1)} %value_gradient.2.refs_4_), channel_id=1, source_target_pairs={{0,24},{8,0},{16,8},{24,16},{1,25},{9,1},{17,9},{25,17},{2,26},{10... | collective-permute-start | bytes 393224 | tf_op jit(solution)/shard_map/ppermute | solution.py:221
  59.7 2.1 %collective-permute-done.8.refs_7_ = bf16[128,512]{1,0:T(8,128)(2,1)S(1)} collective-permute-done((bf16[128,512]{1,0:T(8,128)(2,1)S(1)}, bf16[128,512]{1,0:T(8,128)(2,1)S(1)}, u32[]{:S(2)}, u32[]{:S(2)}) %collective-permute-start.8) | collective-permute-done | bytes 131104 | tf_op jit(solution)/shard_map/ppermute | solution.py:221
  61.7 2.0 %collective-permute-done.7.refs_6_ = bf16[128,512]{1,0:T(8,128)(2,1)S(1)} collective-permute-done((bf16[128,512]{1,0:T(8,128)(2,1)S(1)}, bf16[128,512]{1,0:T(8,128)(2,1)S(1)}, u32[]{:S(2)}, u32[]{:S(2)}) %collective-permute-start.7) | collective-permute-done | bytes 131104 | tf_op jit(solution)/shard_map/ppermute | solution.py:221
  66.9 7.2 %all-to-all-start.1 = ((bf16[16,64,512]{2,1,0:T(8,128)(2,1)}), bf16[16,64,512]{2,1,0:T(8,128)(2,1)}, u32[]{:S(2)}, u32[]{:S(2)}) async-start(bf16[16,64,512]{2,1,0:T(8,128)(2,1)} %bitcast.6), calls=%async_computation.1 | async-start | bytes 2097152 | tf_op jit(solution)/shard_map/all_to_all | solution.py:264
  74.7 2.2 %collective-permute-start.10 = (bf16[128,1024]{1,0:T(8,128)(2,1)S(1)}, bf16[128,1024]{1,0:T(8,128)(2,1)S(1)}, u32[]{:S(2)}, u32[]{:S(2)}) collective-permute-start(bf16[128,1024]{1,0:T(8,128)(2,1)S(1)} %get-tuple-element.42), channel_id=1, source_target_pairs={{0,16},{8,24},{16,0},{24,8},{1,17},{9,25},{17,1},{25,9},{2,18},{10... | collective-permute-start | bytes 786440 | tf_op jit(solution)/shard_map/ppermute | solution.py:221
  76.9 2.0 %collective-permute-start.11 = (bf16[128,1024]{1,0:T(8,128)(2,1)S(1)}, bf16[128,1024]{1,0:T(8,128)(2,1)S(1)}, u32[]{:S(2)}, u32[]{:S(2)}) collective-permute-start(bf16[128,1024]{1,0:T(8,128)(2,1)S(1)} %get-tuple-element.43), channel_id=1, source_target_pairs={{0,24},{8,0},{16,8},{24,16},{1,25},{9,1},{17,9},{25,17},{2,26},{10... | collective-permute-start | bytes 786440 | tf_op jit(solution)/shard_map/ppermute | solution.py:221
  78.9 2.4 %collective-permute-done.9.refs_1_ = bf16[128,1024]{1,0:T(8,128)(2,1)S(1)} collective-permute-done((bf16[128,1024]{1,0:T(8,128)(2,1)S(1)}, bf16[128,1024]{1,0:T(8,128)(2,1)S(1)}, u32[]{:S(2)}, u32[]{:S(2)}) %collective-permute-start.9) | collective-permute-done | bytes 262176 | tf_op jit(solution)/shard_map/ppermute | solution.py:221
  82.0 5.0 %collective-permute-done.10.refs_2_ = bf16[128,1024]{1,0:T(8,128)(2,1)S(1)} collective-permute-done((bf16[128,1024]{1,0:T(8,128)(2,1)S(1)}, bf16[128,1024]{1,0:T(8,128)(2,1)S(1)}, u32[]{:S(2)}, u32[]{:S(2)}) %collective-permute-start.10) | collective-permute-done | bytes 262176 | tf_op jit(solution)/shard_map/ppermute | solution.py:221
  89.1 8.0 %all-to-all-done.1.refs_0_ = bf16[16,64,512]{2,1,0:T(8,128)(2,1)} async-done(((bf16[16,64,512]{2,1,0:T(8,128)(2,1)}), bf16[16,64,512]{2,1,0:T(8,128)(2,1)}, u32[]{:S(2)}, u32[]{:S(2)}) %all-to-all-start.1) | async-done | bytes 1048608 | tf_op jit(solution)/shard_map/all_to_all | solution.py:264
  98.8 30.1 %all_to_all.20 = bf16[16,64,512]{2,1,0:T(8,128)(2,1)S(1)} all-to-all(bf16[16,64,512]{2,1,0:T(8,128)(2,1)S(1)} %get-tuple-element.49), channel_id=1, replica_groups=mesh['yh'=2,'c'=2,'y'=2,'x'=4,'z'=8] {'y','z'}, dimensions={0} | all-to-all | bytes 2097152 | tf_op jit(solution)/shard_map/all_to_all | solution.py:271
  129.7 5.0 %collective-permute-start.13 = (bf16[128,512]{1,0:T(8,128)(2,1)S(1)}, bf16[128,512]{1,0:T(8,128)(2,1)S(1)}, u32[]{:S(2)}, u32[]{:S(2)}) collective-permute-start(bf16[128,512]{1,0:T(8,128)(2,1)S(1)} %get-tuple-element.52), channel_id=1, source_target_pairs={{0,16},{8,24},{16,0},{24,8},{1,17},{9,25},{17,1},{25,9},{2,18},{10... | collective-permute-start | bytes 393224 | tf_op jit(solution)/shard_map/ppermute | solution.py:221
  137.1 4.1 %collective-permute-done.14.refs_3_ = bf16[128,512]{1,0:T(8,128)(2,1)S(1)} collective-permute-done((bf16[128,512]{1,0:T(8,128)(2,1)S(1)}, bf16[128,512]{1,0:T(8,128)(2,1)S(1)}, u32[]{:S(2)}, u32[]{:S(2)}) %collective-permute-start.14) | collective-permute-done | bytes 131104 | tf_op jit(solution)/shard_map/ppermute | solution.py:221
  143.0 2.3 %collective-permute-done.17.refs_7_ = bf16[128,512]{1,0:T(8,128)(2,1)S(1)} collective-permute-done((bf16[128,512]{1,0:T(8,128)(2,1)S(1)}, bf16[128,512]{1,0:T(8,128)(2,1)S(1)}, u32[]{:S(2)}, u32[]{:S(2)}) %collective-permute-start.17) | collective-permute-done | bytes 131104 | tf_op jit(solution)/shard_map/ppermute | solution.py:221
  149.2 33.3 %all_to_all.21.refs_0_ = bf16[16,64,512]{2,1,0:T(8,128)(2,1)S(1)} all-to-all(bf16[16,64,512]{2,1,0:T(8,128)(2,1)S(1)} %bitcast.7), channel_id=1, replica_groups=mesh['yh'=2,'c'=2,'y'=2,'x'=4,'z'=8] {'y','z'}, dimensions={0} | all-to-all | bytes 2097152 | tf_op jit(solution)/shard_map/all_to_all | solution.py:264
  183.4 3.0 %collective-permute-start.18 = (f32[64,512]{1,0:T(8,128)S(1)}, f32[64,512]{1,0:T(8,128)S(1)}, u32[]{:S(2)}, u32[]{:S(2)}) collective-permute-start(f32[64,512]{1,0:T(8,128)S(1)} %get-tuple-element.57), channel_id=1, source_target_pairs={{0,64},{64,0},{1,65},{65,1},{2,66},{66,2},{3,67},{67,3},{4,68},{68... | collective-permute-start | bytes 393224 | tf_op jit(solution)/shard_map/ppermute | solution.py:226
  187.4 2.7 %collective-permute-start.19 = (f32[64,512]{1,0:T(8,128)S(1)}, f32[64,512]{1,0:T(8,128)S(1)}, u32[]{:S(2)}, u32[]{:S(2)}) collective-permute-start(f32[64,512]{1,0:T(8,128)S(1)} %add.12), channel_id=1, source_target_pairs={{0,128},{128,0},{1,129},{129,1},{2,130},{130,2},{3,131},{131,3},{4... | collective-permute-start | bytes 393224 | tf_op jit(solution)/shard_map/ppermute | solution.py:226
  190.1 3.6 %collective-permute-done.19 = f32[64,512]{1,0:T(8,128)S(1)} collective-permute-done((f32[64,512]{1,0:T(8,128)S(1)}, f32[64,512]{1,0:T(8,128)S(1)}, u32[]{:S(2)}, u32[]{:S(2)}) %collective-permute-start.19) | collective-permute-done | bytes 131104 | tf_op jit(solution)/shard_map/ppermute | solution.py:226
  (81 shorter events, 35.8 us)
Async XLA Ops:
  2.8 35.8 %all-to-all-start = ((bf16[16,64,512]{2,1,0:T(8,128)(2,1)}), bf16[16,64,512]{2,1,0:T(8,128)(2,1)S(1)}, u32[]{:S(2)}, u32[]{:S(2)}) async-start(bf16[16,64,512]{2,1,0:T(8,128)(2,1)} %broadcast_in_dim.2), calls=%async_computation | async-start | bytes 2097152 | tf_op jit(solution)/shard_map/all_to_all | solution.py:244
  13.4 8.1 %collective-permute-start = (bf16[128,1024]{1,0:T(8,128)(2,1)S(1)}, bf16[128,1024]{1,0:T(8,128)(2,1)S(1)}, u32[]{:S(2)}, u32[]{:S(2)}) collective-permute-start(bf16[128,1024]{1,0:T(8,128)(2,1)S(1)} %get-tuple-element.31), channel_id=1, source_target_pairs={{0,8},{8,16},{16,24},{24,0},{1,9},{9,17},{17,25},{25,1},{2,10},{10... | collective-permute-start | bytes 786440 | tf_op jit(solution)/shard_map/ppermute | solution.py:221
  14.7 13.5 %collective-permute-start.1 = (bf16[128,1024]{1,0:T(8,128)(2,1)S(1)}, bf16[128,1024]{1,0:T(8,128)(2,1)S(1)}, u32[]{:S(2)}, u32[]{:S(2)}) collective-permute-start(bf16[128,1024]{1,0:T(8,128)(2,1)S(1)} %get-tuple-element.32), channel_id=1, source_target_pairs={{0,16},{8,24},{16,0},{24,8},{1,17},{9,25},{17,1},{25,9},{2,18},{10... | collective-permute-start | bytes 786440 | tf_op jit(solution)/shard_map/ppermute | solution.py:221
  17.2 11.7 %collective-permute-start.2 = (bf16[128,1024]{1,0:T(8,128)(2,1)S(1)}, bf16[128,1024]{1,0:T(8,128)(2,1)S(1)}, u32[]{:S(2)}, u32[]{:S(2)}) collective-permute-start(bf16[128,1024]{1,0:T(8,128)(2,1)S(1)} %get-tuple-element.33), channel_id=1, source_target_pairs={{0,24},{8,0},{16,8},{24,16},{1,25},{9,1},{17,9},{25,17},{2,26},{10... | collective-permute-start | bytes 786440 | tf_op jit(solution)/shard_map/ppermute | solution.py:221
  42.4 13.6 %collective-permute-start.3 = (bf16[128,512]{1,0:T(8,128)(2,1)S(1)}, bf16[128,512]{1,0:T(8,128)(2,1)S(1)}, u32[]{:S(2)}, u32[]{:S(2)}) collective-permute-start(bf16[128,512]{1,0:T(8,128)(2,1)S(1)} %get-tuple-element.35), channel_id=1, source_target_pairs={{0,24},{8,0},{16,8},{24,16},{1,25},{9,1},{17,9},{25,17},{2,26},{10... | collective-permute-start | bytes 393224 | tf_op jit(solution)/shard_map/ppermute | solution.py:221
  44.9 11.1 %collective-permute-start.4 = (bf16[128,512]{1,0:T(8,128)(2,1)S(1)}, bf16[128,512]{1,0:T(8,128)(2,1)S(1)}, u32[]{:S(2)}, u32[]{:S(2)}) collective-permute-start(bf16[128,512]{1,0:T(8,128)(2,1)S(1)} %get-tuple-element.36), channel_id=1, source_target_pairs={{0,16},{8,24},{16,0},{24,8},{1,17},{9,25},{17,1},{25,9},{2,18},{10... | collective-permute-start | bytes 393224 | tf_op jit(solution)/shard_map/ppermute | solution.py:221
  45.4 10.6 %collective-permute-start.5 = (bf16[128,512]{1,0:T(8,128)(2,1)S(1)}, bf16[128,512]{1,0:T(8,128)(2,1)S(1)}, u32[]{:S(2)}, u32[]{:S(2)}) collective-permute-start(bf16[128,512]{1,0:T(8,128)(2,1)S(1)} %get-tuple-element.37), channel_id=1, source_target_pairs={{0,8},{8,16},{16,24},{24,0},{1,9},{9,17},{17,25},{25,1},{2,10},{10... | collective-permute-start | bytes 393224 | tf_op jit(solution)/shard_map/ppermute | solution.py:221
  56.3 5.5 %collective-permute-start.8 = (bf16[128,512]{1,0:T(8,128)(2,1)S(1)}, bf16[128,512]{1,0:T(8,128)(2,1)S(1)}, u32[]{:S(2)}, u32[]{:S(2)}) collective-permute-start(bf16[128,512]{1,0:T(8,128)(2,1)S(1)} %value_gradient.2.refs_4_), channel_id=1, source_target_pairs={{0,24},{8,0},{16,8},{24,16},{1,25},{9,1},{17,9},{25,17},{2,26},{10... | collective-permute-start | bytes 393224 | tf_op jit(solution)/shard_map/ppermute | solution.py:221
  58.4 5.4 %collective-permute-start.7 = (bf16[128,512]{1,0:T(8,128)(2,1)S(1)}, bf16[128,512]{1,0:T(8,128)(2,1)S(1)}, u32[]{:S(2)}, u32[]{:S(2)}) collective-permute-start(bf16[128,512]{1,0:T(8,128)(2,1)S(1)} %value_gradient.2.refs_4_), channel_id=1, source_target_pairs={{0,16},{8,24},{16,0},{24,8},{1,17},{9,25},{17,1},{25,9},{2,18},{10... | collective-permute-start | bytes 393224 | tf_op jit(solution)/shard_map/ppermute | solution.py:221
  59.6 5.5 %collective-permute-start.6 = (bf16[128,512]{1,0:T(8,128)(2,1)S(1)}, bf16[128,512]{1,0:T(8,128)(2,1)S(1)}, u32[]{:S(2)}, u32[]{:S(2)}) collective-permute-start(bf16[128,512]{1,0:T(8,128)(2,1)S(1)} %value_gradient.2.refs_4_), channel_id=1, source_target_pairs={{0,8},{8,16},{16,24},{24,0},{1,9},{9,17},{17,25},{25,1},{2,10},{10... | collective-permute-start | bytes 393224 | tf_op jit(solution)/shard_map/ppermute | solution.py:221
  66.9 30.3 %all-to-all-start.1 = ((bf16[16,64,512]{2,1,0:T(8,128)(2,1)}), bf16[16,64,512]{2,1,0:T(8,128)(2,1)}, u32[]{:S(2)}, u32[]{:S(2)}) async-start(bf16[16,64,512]{2,1,0:T(8,128)(2,1)} %bitcast.6), calls=%async_computation.1 | async-start | bytes 2097152 | tf_op jit(solution)/shard_map/all_to_all | solution.py:264
  74.6 6.7 %collective-permute-start.9 = (bf16[128,1024]{1,0:T(8,128)(2,1)S(1)}, bf16[128,1024]{1,0:T(8,128)(2,1)S(1)}, u32[]{:S(2)}, u32[]{:S(2)}) collective-permute-start(bf16[128,1024]{1,0:T(8,128)(2,1)S(1)} %get-tuple-element.41), channel_id=1, source_target_pairs={{0,8},{8,16},{16,24},{24,0},{1,9},{9,17},{17,25},{25,1},{2,10},{10... | collective-permute-start | bytes 786440 | tf_op jit(solution)/shard_map/ppermute | solution.py:221
  74.7 12.3 %collective-permute-start.10 = (bf16[128,1024]{1,0:T(8,128)(2,1)S(1)}, bf16[128,1024]{1,0:T(8,128)(2,1)S(1)}, u32[]{:S(2)}, u32[]{:S(2)}) collective-permute-start(bf16[128,1024]{1,0:T(8,128)(2,1)S(1)} %get-tuple-element.42), channel_id=1, source_target_pairs={{0,16},{8,24},{16,0},{24,8},{1,17},{9,25},{17,1},{25,9},{2,18},{10... | collective-permute-start | bytes 786440 | tf_op jit(solution)/shard_map/ppermute | solution.py:221
  76.9 11.5 %collective-permute-start.11 = (bf16[128,1024]{1,0:T(8,128)(2,1)S(1)}, bf16[128,1024]{1,0:T(8,128)(2,1)S(1)}, u32[]{:S(2)}, u32[]{:S(2)}) collective-permute-start(bf16[128,1024]{1,0:T(8,128)(2,1)S(1)} %get-tuple-element.43), channel_id=1, source_target_pairs={{0,24},{8,0},{16,8},{24,16},{1,25},{9,1},{17,9},{25,17},{2,26},{10... | collective-permute-start | bytes 786440 | tf_op jit(solution)/shard_map/ppermute | solution.py:221
  97.1 31.7 %copy-start.10 = (bf16[128,1024]{1,0:T(8,128)(2,1)S(1)}, bf16[128,1024]{1,0:T(8,128)(2,1)}, u32[]{:S(2)}) copy-start(bf16[128,1024]{1,0:T(8,128)(2,1)} %copy-done.9) | copy-start | bytes 786436
  129.6 5.9 %collective-permute-start.12 = (bf16[128,512]{1,0:T(8,128)(2,1)S(1)}, bf16[128,512]{1,0:T(8,128)(2,1)S(1)}, u32[]{:S(2)}, u32[]{:S(2)}) collective-permute-start(bf16[128,512]{1,0:T(8,128)(2,1)S(1)} %get-tuple-element.51), channel_id=1, source_target_pairs={{0,24},{8,0},{16,8},{24,16},{1,25},{9,1},{17,9},{25,17},{2,26},{10... | collective-permute-start | bytes 393224 | tf_op jit(solution)/shard_map/ppermute | solution.py:221
  129.7 7.4 %collective-permute-start.13 = (bf16[128,512]{1,0:T(8,128)(2,1)S(1)}, bf16[128,512]{1,0:T(8,128)(2,1)S(1)}, u32[]{:S(2)}, u32[]{:S(2)}) collective-permute-start(bf16[128,512]{1,0:T(8,128)(2,1)S(1)} %get-tuple-element.52), channel_id=1, source_target_pairs={{0,16},{8,24},{16,0},{24,8},{1,17},{9,25},{17,1},{25,9},{2,18},{10... | collective-permute-start | bytes 393224 | tf_op jit(solution)/shard_map/ppermute | solution.py:221
  134.7 6.4 %collective-permute-start.14 = (bf16[128,512]{1,0:T(8,128)(2,1)S(1)}, bf16[128,512]{1,0:T(8,128)(2,1)S(1)}, u32[]{:S(2)}, u32[]{:S(2)}) collective-permute-start(bf16[128,512]{1,0:T(8,128)(2,1)S(1)} %get-tuple-element.53), channel_id=1, source_target_pairs={{0,8},{8,16},{16,24},{24,0},{1,9},{9,17},{17,25},{25,1},{2,10},{10... | collective-permute-start | bytes 393224 | tf_op jit(solution)/shard_map/ppermute | solution.py:221
  141.4 3.9 %collective-permute-start.17 = (bf16[128,512]{1,0:T(8,128)(2,1)S(1)}, bf16[128,512]{1,0:T(8,128)(2,1)S(1)}, u32[]{:S(2)}, u32[]{:S(2)}) collective-permute-start(bf16[128,512]{1,0:T(8,128)(2,1)S(1)} %value_gradient.3.refs_4_), channel_id=1, source_target_pairs={{0,24},{8,0},{16,8},{24,16},{1,25},{9,1},{17,9},{25,17},{2,26},{10... | collective-permute-start | bytes 393224 | tf_op jit(solution)/shard_map/ppermute | solution.py:221
  141.8 5.4 %collective-permute-start.16 = (bf16[128,512]{1,0:T(8,128)(2,1)S(1)}, bf16[128,512]{1,0:T(8,128)(2,1)S(1)}, u32[]{:S(2)}, u32[]{:S(2)}) collective-permute-start(bf16[128,512]{1,0:T(8,128)(2,1)S(1)} %value_gradient.3.refs_4_), channel_id=1, source_target_pairs={{0,16},{8,24},{16,0},{24,8},{1,17},{9,25},{17,1},{25,9},{2,18},{10... | collective-permute-start | bytes 393224 | tf_op jit(solution)/shard_map/ppermute | solution.py:221
  142.4 6.1 %collective-permute-start.15 = (bf16[128,512]{1,0:T(8,128)(2,1)S(1)}, bf16[128,512]{1,0:T(8,128)(2,1)S(1)}, u32[]{:S(2)}, u32[]{:S(2)}) collective-permute-start(bf16[128,512]{1,0:T(8,128)(2,1)S(1)} %value_gradient.3.refs_4_), channel_id=1, source_target_pairs={{0,8},{8,16},{16,24},{24,0},{1,9},{9,17},{17,25},{25,1},{2,10},{10... | collective-permute-start | bytes 393224 | tf_op jit(solution)/shard_map/ppermute | solution.py:221
  149.2 44.5 %copy-start.21 = (f32[64,512]{1,0:T(8,128)S(1)}, f32[64,512]{1,0:T(8,128)}, u32[]{:S(2)}) copy-start(f32[64,512]{1,0:T(8,128)} %param.11) | copy-start | bytes 393220
  183.4 3.9 %collective-permute-start.18 = (f32[64,512]{1,0:T(8,128)S(1)}, f32[64,512]{1,0:T(8,128)S(1)}, u32[]{:S(2)}, u32[]{:S(2)}) collective-permute-start(f32[64,512]{1,0:T(8,128)S(1)} %get-tuple-element.57), channel_id=1, source_target_pairs={{0,64},{64,0},{1,65},{65,1},{2,66},{66,2},{3,67},{67,3},{4,68},{68... | collective-permute-start | bytes 393224 | tf_op jit(solution)/shard_map/ppermute | solution.py:226
  187.4 6.3 %collective-permute-start.19 = (f32[64,512]{1,0:T(8,128)S(1)}, f32[64,512]{1,0:T(8,128)S(1)}, u32[]{:S(2)}, u32[]{:S(2)}) collective-permute-start(f32[64,512]{1,0:T(8,128)S(1)} %add.12), channel_id=1, source_target_pairs={{0,128},{128,0},{1,129},{129,1},{2,130},{130,2},{3,131},{131,3},{4... | collective-permute-start | bytes 393224 | tf_op jit(solution)/shard_map/ppermute | solution.py:226
  (20 other events, 166.7 us)

commit v2 on v1

v2 whole, which is shorter than its diff:
```python
import math

import jax
import jax.numpy as jnp
from jax import lax
from jax.experimental import pallas as pl
from jax.experimental.pallas import tpu as pltpu
from jax.sharding import Mesh
from jax.sharding import PartitionSpec as P

D = 4096
QH = 32
KVH = 4
HD = 128
GROUP = QH // KVH
FSDP = ("y", "x", "z")
REPLICA = ("yh", "c")
ALL = ("yh", "c", "y", "x", "z")

beta_one = 0.9
beta_two = 0.95
inner_rate = 0.05
decay_rate = 0.1
outer_rate = 0.7
outer_mu = 0.9

F32 = jnp.float32
BF16 = jnp.bfloat16
PARAMS = pltpu.CompilerParams(vmem_limit_bytes=12 << 20)


SMEM_SPEC = pl.BlockSpec(memory_space=pltpu.SMEM)
VMEM_SPEC = pl.BlockSpec(memory_space=pltpu.VMEM)
HBM_SPEC = pl.BlockSpec(memory_space=pltpu.HBM)
ANY_SPEC = pl.BlockSpec(memory_space=pl.ANY)


def without(body, at, count):
    return lambda *refs: body(*refs[:at], *refs[at + count :])


def shape_of(shape, dtype):
    return jax.ShapeDtypeStruct(shape, dtype)


def attention_body(
    place_ref, q_hbm, k_hbm, t_hbm, out_ref, q_ref, k_ref, t_ref, p_ref, sems, *, step
):
    heads, length, wide = q_ref.shape
    copies = []
    for g in range(heads):
        cols = pl.ds(g * wide, wide)
        near = pl.ds(g * HD, HD)
        copies.append(
            (
                pltpu.make_async_copy(q_hbm.at[step, :, cols], q_ref.at[g], sems.at[g, 0]),
                pltpu.make_async_copy(k_hbm.at[step, :, near], k_ref.at[g], sems.at[g, 1]),
                pltpu.make_async_copy(t_hbm.at[step, :, cols], t_ref.at[g], sems.at[g, 2]),
            )
        )
        for copy in copies[g]:
            copy.start()
    row = lax.broadcasted_iota(jnp.int32, (length, length), 0)
    col = lax.broadcasted_iota(jnp.int32, (length, length), 1)
    causal = row >= col
    shift = place_ref[0] * (heads // 2)
    for g in range(heads):
        for copy in copies[g]:
            copy.wait()
        keys = k_ref[g]
        for j in range(GROUP):
            head = q_ref[g, :, j * HD : (j + 1) * HD]
            scores = lax.dot_general(
                head, keys, (((1,), (1,)), ((), ())), preferred_element_type=F32
            )
            scores = jnp.where(causal, scores / math.sqrt(HD), -1e30)
            expd = jnp.exp(scores - jnp.max(scores, axis=-1, keepdims=True))
            attention = expd / jnp.sum(expd, axis=-1, keepdims=True)
            rows = slice(j * length, (j + 1) * length)
            p_ref[rows, :length] = attention.astype(BF16)
            p_ref[rows, length:] = t_ref[g, :, j * HD : (j + 1) * HD]
        both = p_ref[...]
        out_ref[lax.rem(g + shift, heads)] = lax.dot_general(
            both[:, :length], both, (((0,), (0,)), ((), ())), preferred_element_type=F32
        )


def attention_sums(place, queries, keys, targets, step, after):
    length = queries.shape[1]
    wide = GROUP * HD
    return pl.pallas_call(
        without(lambda *refs: attention_body(*refs, step=step), 4, len(after)),
        in_specs=[SMEM_SPEC] + [HBM_SPEC] * 3 + [ANY_SPEC] * len(after),
        out_shape=shape_of((KVH, length, length + HD), F32),
        scratch_shapes=[
            pltpu.VMEM((KVH, length, wide), BF16),
            pltpu.VMEM((KVH, length, HD), BF16),
            pltpu.VMEM((KVH, length, wide), BF16),
            pltpu.VMEM((GROUP * length, length + HD), BF16),
            pltpu.SemaphoreType.DMA((KVH, 3)),
        ],
        compiler_params=PARAMS,
        cost_estimate=pl.CostEstimate(flops=2 << 30, transcendentals=1 << 19, bytes_accessed=1 << 10),
        name="attention_sums",
    )(place, queries, keys, targets, *after)


def slab_body(place_ref, in_hbm, *refs, step, ys, xs, shifts):
    outs, sems = refs[:-1], refs[-1]
    wide = outs[0].shape[1] // ys
    copies = []
    for i, k in enumerate(shifts):
        for y in range(ys):
            start = pl.multiple_of((y * xs + lax.rem(place_ref[0] + k, xs)) * wide, wide)
            copies.append(
                pltpu.make_async_copy(
                    in_hbm.at[step, :, pl.ds(start, wide)],
                    outs[i].at[:, pl.ds(y * wide, wide)],
                    sems.at[i, y],
                )
            )
            copies[-1].start()
    for copy in copies:
        copy.wait()


def slabs_of(place, layer_input, step, ys, xs, shifts, after):
    _, length, width = layer_input.shape
    count = len(shifts)
    body = lambda *refs: slab_body(*refs, step=step, ys=ys, xs=xs, shifts=shifts)
    return list(
        pl.pallas_call(
            without(body, 2, len(after)),
            in_specs=[SMEM_SPEC, HBM_SPEC] + [ANY_SPEC] * len(after),
            out_specs=[HBM_SPEC] * count,
            out_shape=[shape_of((length, width // xs), BF16)] * count,
            scratch_shapes=[pltpu.SemaphoreType.DMA((count, ys))],
            compiler_params=PARAMS,
            cost_estimate=pl.CostEstimate(flops=1 << 30, transcendentals=0, bytes_accessed=1 << 10),
            name="slabs",
        )(place, layer_input, *after)
    )


def nothing_body(value_ref, after_ref, out_ref):
    pass


def passed_after(value, after):
    return pl.pallas_call(
        nothing_body,
        in_specs=[ANY_SPEC, ANY_SPEC],
        out_specs=ANY_SPEC,
        out_shape=shape_of(value.shape, value.dtype),
        input_output_aliases={0: 0},
        compiler_params=PARAMS,
        name="passed_after",
    )(value, after)


def values_body(*refs):
    x_refs, w_ref, out_refs = refs[:8], refs[8], refs[9:]
    zs, ys = w_ref.shape[:2]
    weights = jnp.concatenate([w_ref[z, y] for y in range(ys) for z in range(zs)], axis=0)
    for seq in range(2):
        for k in range(4):
            part = jnp.dot(x_refs[4 * seq + k][...], weights, preferred_element_type=F32)
            out = out_refs[k]
            out[seq] = (part * (1.0 / math.sqrt(D))).astype(out.dtype)


def partial_values(slabs, gathered):
    length = slabs[0].shape[0]
    columns = gathered.shape[-1]
    shape = (2, length, columns)
    return pl.pallas_call(
        values_body,
        out_shape=[shape_of(shape, F32)] + [shape_of(shape, BF16)] * 3,
        compiler_params=PARAMS,
        name="partial_values",
    )(*slabs, gathered)


def value_grad_body(v0, v1, v2, v3, own_ref, other_ref, out_ref, *, tok_rep):
    length = v0.shape[1]
    for seq, sums in enumerate((own_ref, other_ref)):
        total = (v0[seq] + v1[seq].astype(F32)) + (v2[seq].astype(F32) + v3[seq].astype(F32))
        values = total.astype(BF16)
        for h in range(sums.shape[0]):
            m = sums[h, :, :length]
            n = sums[h, :, length:]
            high = m.astype(BF16)
            low = (m - high.astype(F32)).astype(BF16)
            cols = slice(h * HD, (h + 1) * HD)
            part = values[:, cols]
            attended = jnp.dot(high, part, preferred_element_type=F32) + jnp.dot(
                low, part, preferred_element_type=F32
            )
            out_ref[seq, :, cols] = ((attended - n) * (1.0 / tok_rep)).astype(BF16)


def value_gradient(parts, own, other, tok_rep, after):
    return pl.pallas_call(
        without(lambda *refs: value_grad_body(*refs, tok_rep=tok_rep), 6, len(after)),
        in_specs=[VMEM_SPEC] * 6 + [ANY_SPEC] * len(after),
        out_shape=shape_of(parts[0].shape, BF16),
        compiler_params=PARAMS,
        name="value_gradient",
    )(*parts, own, other, *after)


def gradient_body(*refs):
    x_refs, g_refs, out_ref = refs[:8], refs[8:12], refs[12]
    zs, ys, rows = out_ref.shape[:3]
    inputs = jnp.concatenate([r[...] for r in x_refs], axis=0)
    grads = jnp.concatenate([g_refs[k][seq] for seq in range(2) for k in range(4)], axis=0)
    total = lax.dot_general(inputs, grads, (((0,), (0,)), ((), ())), preferred_element_type=F32)
    total = (total * (1.0 / math.sqrt(D))).astype(BF16)
    for y in range(ys):
        for z in range(zs):
            start = (y * zs + z) * rows
            out_ref[z, y] = total[start : start + rows]


def partial_gradient(slabs, grads, zs, ys):
    width = slabs[0].shape[1]
    columns = grads[0].shape[-1]
    return pl.pallas_call(
        gradient_body,
        out_shape=shape_of((zs, ys, width // (zs * ys), columns), BF16),
        compiler_params=PARAMS,
        name="partial_gradient",
    )(*slabs, *grads)


def adam_body(*refs, step, floor, last):
    if step == 0:
        recv, theta_ref, m_out, u_out, theta_out, sent = refs
    else:
        recv, theta_ref, m_ref, u_ref, start_ref, m_out, u_out, theta_out, sent = refs
    gradient = recv[0].astype(F32)
    for z in range(1, recv.shape[0]):
        gradient = gradient + recv[z].astype(F32)
    moment_one = (1.0 - beta_one) * gradient
    moment_two = (1.0 - beta_two) * gradient * gradient
    if step > 0:
        moment_one = beta_one * m_ref[...] + moment_one
        moment_two = beta_two * u_ref[...] + moment_two
    corrected_one = moment_one / (1.0 - beta_one ** (step + 1))
    corrected_two = moment_two / (1.0 - beta_two ** (step + 1))
    theta = theta_ref[...]
    theta = theta - inner_rate * (
        corrected_one / (jnp.sqrt(corrected_two) + floor) + decay_rate * theta
    )
    m_out[...] = moment_one
    u_out[...] = moment_two
    theta_out[...] = theta
    if last:
        sent[...] = start_ref[...] - theta
    else:
        rounded = theta.astype(BF16)
        for z in range(recv.shape[0]):
            sent[z] = rounded


def adam(received, state, step, floor, last, after):
    shape = received.shape[1:]
    sent = shape_of(shape, F32) if last else shape_of(received.shape, BF16)
    return pl.pallas_call(
        without(
            lambda *refs: adam_body(*refs, step=step, floor=floor, last=last),
            1 + len(state),
            len(after),
        ),
        in_specs=[VMEM_SPEC] * (1 + len(state)) + [ANY_SPEC] * len(after),
        out_shape=[shape_of(shape, F32)] * 3 + [sent],
        compiler_params=PARAMS,
        name="adam",
    )(received, *state, *after)


def shifted(value, axis, k):
    size = lax.axis_size(axis)
    return lax.ppermute(value, axis, [(i, (i + k) % size) for i in range(size)])


def flipped(value, axis, mask):
    size = lax.axis_size(axis)
    return lax.ppermute(value, axis, [(i, i ^ mask) for i in range(size)])


def pick(value, index, size, axis):
    return lax.dynamic_slice_in_dim(value, index * size, size, axis)


def shards(layer_input, queries, keys, targets, value_weight, outer_momentum):
    inner_steps, length, width = layer_input.shape
    shard_rows, columns = value_weight.shape
    half = columns // 2
    ys, xs, zs = (lax.axis_size(a) for a in FSDP)
    tok_rep = length * ys * xs * zs
    replicas = lax.axis_size(REPLICA)
    floor = math.sqrt(GROUP / (tok_rep * D))
    core, y = lax.axis_index("c"), lax.axis_index("y")
    x_place = lax.axis_index("x").astype(jnp.int32).reshape(1)
    y_place = y.astype(jnp.int32).reshape(1)

    def swapped(slab, k):
        pairs = [
            ((a * 2 + b) * xs + i, (b * 2 + a) * xs + (i + k) % xs)
            for a in range(2)
            for b in range(2)
            for i in range(xs)
        ]
        return lax.ppermute(slab, ("c", "y", "x"), pairs)

    def both_cores(own):
        return own + [flipped(slab, "c", 1) for slab in own]

    def sums_of(sums):
        heads = KVH // 2
        pairs = [(a, b) for a in range(2) for b in range(2)]
        own = [(a * 2 + b, b * 2 + a) for a, b in pairs]
        other = [(a * 2 + b, (1 - b) * 2 + a) for a, b in pairs]
        return (
            lax.ppermute(sums[:heads], ("c", "y"), own),
            lax.ppermute(sums[heads:], ("c", "y"), other),
        )

    every = tuple(range(xs))
    raw = slabs_of(x_place, layer_input, 0, ys, xs, every, ())
    own_slabs = [swapped(slab, k) for k, slab in enumerate(raw)]
    own_half = pick(value_weight, core, half, 1)
    first = own_half.astype(BF16)
    gathered = lax.all_to_all(
        jnp.broadcast_to(first[None], (zs * ys, *first.shape)), ("z", "y"), 0, 0, tiled=True
    ).reshape(zs, ys, shard_rows, half)
    sums = attention_sums(y_place, queries, keys, targets, 0, raw[:1])
    own_slabs = [passed_after(slab, sums) for slab in own_slabs]
    sums = sums_of(sums)
    slabs = both_cores(own_slabs)
    far_half = flipped(own_half, "y", 1)
    start = jnp.where(y == 0, jnp.stack([own_half, far_half]), jnp.stack([far_half, own_half]))

    theta = start
    state = ()
    for step in range(inner_steps):
        last = step == inner_steps - 1
        parts = list(partial_values(slabs, gathered))
        after = []
        if not last:
            head = parts[:1]
            later = attention_sums(y_place, queries, keys, targets, step + 1, head)
            moved = slabs_of(x_place, layer_input, step + 1, ys, xs, every[:1], head)
            after = [later, *moved]
        parts = [parts[0]] + [shifted(parts[k], "x", -k) for k in range(1, xs)]
        grad = value_gradient(parts, *sums, tok_rep, after)
        grads = [grad] + [shifted(grad, "x", k) for k in range(1, xs)]
        scattered = partial_gradient(slabs, grads, zs, ys)
        after = []
        if not last:
            sums = sums_of(later)
            moved += slabs_of(x_place, layer_input, step + 1, ys, xs, every[1:], [scattered])
            moved = [swapped(slab, k) for k, slab in enumerate(moved)]
            after = [*sums, *moved[:2]]
        received = lax.all_to_all(scattered, "z", 0, 0, tiled=True)
        args = (theta,) if step == 0 else (theta, *state, start)
        m, u, theta, sent = adam(received, args, step, floor, last, after)
        state = (m, u)
        if not last:
            gathered = lax.all_to_all(sent, "z", 0, 0, tiled=True)
            slabs = both_cores(moved)

    near = lax.dynamic_index_in_dim(sent, y, 0, False)
    far = lax.dynamic_index_in_dim(sent, 1 - y, 0, False)
    total = (near + flipped(far, ("yh", "y"), 1)) + (
        flipped(near, ("yh", "y"), 2) + flipped(far, ("yh", "y"), 3)
    )
    mean_half = total / replicas
    mean_other = flipped(mean_half, "c", 1)
    mean_delta = jnp.where(
        core == 0,
        jnp.concatenate([mean_half, mean_other], axis=1),
        jnp.concatenate([mean_other, mean_half], axis=1),
    )
    new_momentum = outer_mu * outer_momentum + mean_delta
    new_weight = value_weight - outer_rate * (mean_delta + outer_mu * new_momentum)
    return (new_weight, new_momentum)


def solution(mesh):
    split = Mesh(mesh.devices.reshape(2, 2, 2, 4, 8), ALL)
    tokens = P(None, REPLICA + FSDP, None)
    in_specs = (tokens, tokens, tokens, tokens, P(FSDP, None), P(FSDP, None))
    out_specs = (P(FSDP, None), P(FSDP, None))
    return jax.shard_map(
        shards, mesh=split, in_specs=in_specs, out_specs=out_specs, check_vma=False
    )
```

time: 195 us -> 176 us (0.903)
  blocking collectives: 63.4 us -> 0 us
  starting transfers between devices: 46.7 us -> 79.5 us
  waiting for transfers between devices: 55.6 us -> 67.5 us
  local copies, waits for them, and re-layouts: 11.9 us -> 9.71 us
    all_to_all x2 -> x0, blocking collectives: 63.4 us -> none  [the longest x1 33.3 us: shards(): received = lax.all_to_all(scattered, OWNERS, 0, 0, tiled=True)]
    ppermute x0 -> x12, starting transfers between devices: none -> 24.3 us  [the longest x8 18.3 us: swapped(): return lax.ppermute(slab, ('c', 'y', 'x'), pairs)]
    ppermute x0 -> x12, waiting for transfers between devices: none -> 16 us  [the longest x8 16 us: swapped(): return lax.ppermute(slab, ('c', 'y', 'x'), pairs)]
    all_to_all x2 -> x4, starting transfers between devices: 17.3 us -> 30.5 us  [the longest x2 13.3 us: shards(): received = lax.all_to_all(scattered, 'z', 0, 0, tiled=True)]
    ppermute x18 -> x12, starting transfers between devices: 23.7 us -> 12.1 us  [shifted(): return lax.ppermute(value, axis, [(i, (i + k) % size) for i in range(size)])]
    ppermute x18 -> x12, waiting for transfers between devices: 33.9 us -> 23.8 us  [shifted(): return lax.ppermute(value, axis, [(i, (i + k) % size) for i in range(size)])]
    ppermute x2 -> x13, waiting for transfers between devices: 4.61 us -> 12.1 us  [flipped(): return lax.ppermute(value, axis, [(i, i ^ mask) for i in range(size)])]
    ppermute x2 -> x13, starting transfers between devices: 5.65 us -> 12.6 us  [flipped(): return lax.ppermute(value, axis, [(i, i ^ mask) for i in range(size)])]
  transfers between devices with their start and end apart: 22 -> 41, of which waited for: 17 -> 18; matrix products, arithmetic and copies ran while one was open for 0% -> 0% of each run, Pallas kernels for 4% -> 5%
where the time goes in v2:
time: 176 us; the launch traced here: 175 us
  starting transfers between devices  79.5 us (45%)
  waiting for transfers between devices  67.5 us (38%)
  Pallas kernels  15.1 us (9%)
  local copies, waits for them, and re-layouts  9.71 us (6%)
  other arithmetic  2.24 us (1%)
    ppermute x12, waiting for transfers between devices, shifted(): return lax.ppermute(value, axis, [(i, (i + k) % size) for i in range(size)])  23.8 us
    ppermute x8, starting transfers between devices, swapped(): return lax.ppermute(slab, ('c', 'y', 'x'), pairs)  18.3 us
    ppermute x8, waiting for transfers between devices, swapped(): return lax.ppermute(slab, ('c', 'y', 'x'), pairs)  16 us
    all_to_all x2, waiting for transfers between devices, shards(): received = lax.all_to_all(scattered, 'z', 0, 0, tiled=True)  15.6 us
    all_to_all x2, starting transfers between devices, shards(): received = lax.all_to_all(scattered, 'z', 0, 0, tiled=True)  13.3 us
    ppermute x13, starting transfers between devices, flipped(): return lax.ppermute(value, axis, [(i, i ^ mask) for i in range(size)])  12.6 us
    ppermute x13, waiting for transfers between devices, flipped(): return lax.ppermute(value, axis, [(i, i ^ mask) for i in range(size)])  12.1 us
    ppermute x12, starting transfers between devices, shifted(): return lax.ppermute(value, axis, [(i, (i + k) % size) for i in range(size)])  12.1 us
  transfers between devices with their start and end apart: 41, of which 18 were waited for; matrix products, arithmetic and copies ran while one was open for 0% of the time, Pallas kernels for 5%

profile of v2, /device:TPU:1, one launch (start us, length us, event | category | flops | bytes accessed | tf_op | source)
XLA Modules:
  0.0 175.0 jit_solution(9663143852031852771)
XLA Ops:
  3.0 10.3 %all-to-all-start = ((bf16[16,64,256]{2,1,0:T(8,128)(2,1)}), bf16[16,64,256]{2,1,0:T(8,128)(2,1)S(1)}, u32[]{:S(2)}, u32[]{:S(2)}) async-start(bf16[16,64,256]{2,1,0:T(8,128)(2,1)} %broadcast_in_dim.2), calls=%async_computation | async-start | bytes 1048576 | tf_op jit(solution)/shard_map/all_to_all | solution.py:335
  15.1 4.4 %collective-permute-start = (bf16[128,1024]{1,0:T(8,128)(2,1)S(1)}, bf16[128,1024]{1,0:T(8,128)(2,1)S(1)}, u32[]{:S(2)}, u32[]{:S(2)}) collective-permute-start(bf16[128,1024]{1,0:T(8,128)(2,1)S(1)} %get-tuple-element.22.refs_4_), channel_id=1, source_target_pairs={{0,0},{8,8},{16,16},{24,24},{32,64},{40,72},{48,80},{56,88},{64,32... | collective-permute-start | bytes 786440 | tf_op jit(solution)/shard_map/ppermute | solution.py:315
  20.6 3.9 %collective-permute-start.2 = (bf16[128,1024]{1,0:T(8,128)(2,1)S(1)}, bf16[128,1024]{1,0:T(8,128)(2,1)S(1)}, u32[]{:S(2)}, u32[]{:S(2)}) collective-permute-start(bf16[128,1024]{1,0:T(8,128)(2,1)S(1)} %get-tuple-element.24), channel_id=1, source_target_pairs={{0,16},{8,24},{16,0},{24,8},{32,80},{40,88},{48,64},{56,72},{64,48... | collective-permute-start | bytes 786440 | tf_op jit(solution)/shard_map/ppermute | solution.py:315
  28.5 3.8 %attention_sums.2.after_ref = f32[4,128,256]{2,1,0:T(8,128)S(1)} custom-call(s32[1]{0:T(128)} %bitcast.1.refs_0_, bf16[2,128,4096]{2,1,0:T(8,128)(2,1)S(1)} %copy-done.2, bf16[2,128,512]{2,1,0:T(8,128)(2,1)S(1)} %copy-done.9, bf16[2,128,4096]{2,1,0:T(8,128)(2,1)S(1)} %copy-done.4, bf16[128,1024]{1,0:T(8,128)(2,1)S(1)} %get-tuple-element.22.refs_4_), custom_call_target="tpu_custom_call" | custom-call | flops 2147483648 | bytes 1024 | tf_op jit(solution)/shard_map/attention_sums/pallas_call | solution.py:91
  32.3 3.2 %collective-permute-done.value_ref = bf16[128,1024]{1,0:T(8,128)(2,1)S(1)} collective-permute-done((bf16[128,1024]{1,0:T(8,128)(2,1)S(1)}, bf16[128,1024]{1,0:T(8,128)(2,1)S(1)}, u32[]{:S(2)}, u32[]{:S(2)}) %collective-permute-start) | collective-permute-done | bytes 262176 | tf_op jit(solution)/shard_map/ppermute | solution.py:315
  37.8 3.9 %collective-permute-start.12 = (f32[2,128,256]{2,1,0:T(8,128)}, f32[2,128,256]{2,1,0:T(8,128)S(1)}, u32[]{:S(2)}, u32[]{:S(2)}) collective-permute-start(f32[2,128,256]{2,1,0:T(8,128)} %get-tuple-element.49), channel_id=1, source_target_pairs={{0,0},{32,64},{64,32},{96,96},{1,1},{33,65},{65,33},{97,97},{2,2},... | collective-permute-start | bytes 786440 | tf_op jit(solution)/shard_map/ppermute | solution.py:326
  42.6 2.6 %collective-permute-start.9 = (bf16[2,128,256]{2,1,0:T(8,128)(2,1)S(1)}, bf16[2,128,256]{2,1,0:T(8,128)(2,1)S(1)}, u32[]{:S(2)}, u32[]{:S(2)}) collective-permute-start(bf16[2,128,256]{2,1,0:T(8,128)(2,1)S(1)} %get-tuple-element.27), channel_id=1, source_target_pairs={{0,24},{8,0},{16,8},{24,16},{1,25},{9,1},{17,9},{25,17},{2,26},{10... | collective-permute-start | bytes 393224 | tf_op jit(solution)/shard_map/ppermute | solution.py:284
  47.9 3.7 %attention_sums.3.refs_6_ = f32[4,128,256]{2,1,0:T(8,128)S(1)} custom-call(s32[1]{0:T(128)} %bitcast.1.refs_0_, bf16[2,128,4096]{2,1,0:T(8,128)(2,1)S(1)} %copy-done.3, bf16[2,128,512]{2,1,0:T(8,128)(2,1)S(1)} %copy-done.9, bf16[2,128,4096]{2,1,0:T(8,128)(2,1)S(1)} %copy-done.5, f32[2,128,256]{2,1,0:T(8,128)S(1)} %get-tuple-element.26.refs_2_.refs_4_.refs_0_), custom_call_target="tpu_custom_call" | custom-call | flops 2147483648 | bytes 1024 | tf_op jit(solution)/shard_map/attention_sums/pallas_call | solution.py:91
  51.8 3.1 %collective-permute-done.11.refs_3_ = bf16[2,128,256]{2,1,0:T(8,128)(2,1)S(1)} collective-permute-done((bf16[2,128,256]{2,1,0:T(8,128)(2,1)S(1)}, bf16[2,128,256]{2,1,0:T(8,128)(2,1)S(1)}, u32[]{:S(2)}, u32[]{:S(2)}) %collective-permute-start.11) | collective-permute-done | bytes 131104 | tf_op jit(solution)/shard_map/ppermute | solution.py:284
  57.9 6.2 %collective-permute-done.14.refs_9_ = bf16[2,128,256]{2,1,0:T(8,128)(2,1)S(1)} collective-permute-done((bf16[2,128,256]{2,1,0:T(8,128)(2,1)S(1)}, bf16[2,128,256]{2,1,0:T(8,128)(2,1)S(1)}, u32[]{:S(2)}, u32[]{:S(2)}) %collective-permute-start.14) | collective-permute-done | bytes 131104 | tf_op jit(solution)/shard_map/ppermute | solution.py:284
  65.8 6.4 %all-to-all-start.1 = ((bf16[8,2,64,256]{3,2,1,0:T(8,128)(2,1)}), bf16[8,2,64,256]{3,2,1,0:T(8,128)(2,1)S(1)}, u32[]{:S(2)}, u32[]{:S(2)}) async-start(bf16[8,2,64,256]{3,2,1,0:T(8,128)(2,1)} %partial_gradient.2.refs_2_), calls=%async_computation.1 | async-start | bytes 1048576 | tf_op jit(solution)/shard_map/all_to_all | solution.py:366
  72.1 3.9 %collective-permute-start.8 = (bf16[128,1024]{1,0:T(8,128)(2,1)S(1)}, bf16[128,1024]{1,0:T(8,128)(2,1)S(1)}, u32[]{:S(2)}, u32[]{:S(2)}) collective-permute-start(bf16[128,1024]{1,0:T(8,128)(2,1)S(1)} %slabs.4.refs_7_), channel_id=1, source_target_pairs={{0,0},{8,8},{16,16},{24,24},{32,64},{40,72},{48,80},{56,88},{64,32... | collective-permute-start | bytes 786440 | tf_op jit(solution)/shard_map/ppermute | solution.py:315
  81.9 6.3 %collective-permute-done.24 = f32[64,256]{1,0:T(8,128)S(1)} collective-permute-done((f32[64,256]{1,0:T(8,128)S(1)}, f32[64,256]{1,0:T(8,128)S(1)}, u32[]{:S(2)}, u32[]{:S(2)}) %collective-permute-start.24) | collective-permute-done | bytes 65568 | tf_op jit(solution)/shard_map/ppermute | solution.py:289
  88.3 2.3 %collective-permute-done.17.refs_5_.refs_1_ = bf16[128,1024]{1,0:T(8,128)(2,1)S(1)} collective-permute-done((bf16[128,1024]{1,0:T(8,128)(2,1)S(1)}, bf16[128,1024]{1,0:T(8,128)(2,1)S(1)}, u32[]{:S(2)}, u32[]{:S(2)}) %collective-permute-start.17) | collective-permute-done | bytes 262176 | tf_op jit(solution)/shard_map/ppermute | solution.py:315
  91.6 6.9 %all-to-all-start.2 = ((bf16[8,2,64,256]{3,2,1,0:T(8,128)(2,1)}), bf16[8,2,64,256]{3,2,1,0:T(8,128)(2,1)S(1)}, u32[]{:S(2)}, u32[]{:S(2)}) async-start(bf16[8,2,64,256]{3,2,1,0:T(8,128)(2,1)} %get-tuple-element.33), calls=%async_computation.2 | async-start | bytes 1048576 | tf_op jit(solution)/shard_map/all_to_all | solution.py:371
  102.7 6.1 %collective-permute-done.18.refs_2_ = bf16[128,1024]{1,0:T(8,128)(2,1)S(1)} collective-permute-done((bf16[128,1024]{1,0:T(8,128)(2,1)S(1)}, bf16[128,1024]{1,0:T(8,128)(2,1)S(1)}, u32[]{:S(2)}, u32[]{:S(2)}) %collective-permute-start.18) | collective-permute-done | bytes 262176 | tf_op jit(solution)/shard_map/ppermute | solution.py:315
  110.2 3.5 %collective-permute-done.19.refs_3_ = bf16[128,1024]{1,0:T(8,128)(2,1)S(1)} collective-permute-done((bf16[128,1024]{1,0:T(8,128)(2,1)S(1)}, bf16[128,1024]{1,0:T(8,128)(2,1)S(1)}, u32[]{:S(2)}, u32[]{:S(2)}) %collective-permute-start.19) | collective-permute-done | bytes 262176 | tf_op jit(solution)/shard_map/ppermute | solution.py:315
  119.5 4.8 %collective-permute-done.27.refs_1_ = bf16[2,128,256]{2,1,0:T(8,128)(2,1)S(1)} collective-permute-done((bf16[2,128,256]{2,1,0:T(8,128)(2,1)S(1)}, bf16[2,128,256]{2,1,0:T(8,128)(2,1)S(1)}, u32[]{:S(2)}, u32[]{:S(2)}) %collective-permute-start.27) | collective-permute-done | bytes 131104 | tf_op jit(solution)/shard_map/ppermute | solution.py:284
  124.8 3.2 %collective-permute-done.29.refs_3_ = bf16[2,128,256]{2,1,0:T(8,128)(2,1)S(1)} collective-permute-done((bf16[2,128,256]{2,1,0:T(8,128)(2,1)S(1)}, bf16[2,128,256]{2,1,0:T(8,128)(2,1)S(1)}, u32[]{:S(2)}, u32[]{:S(2)}) %collective-permute-start.29) | collective-permute-done | bytes 131104 | tf_op jit(solution)/shard_map/ppermute | solution.py:284
  130.9 6.0 %collective-permute-done.30.refs_9_ = bf16[2,128,256]{2,1,0:T(8,128)(2,1)S(1)} collective-permute-done((bf16[2,128,256]{2,1,0:T(8,128)(2,1)S(1)}, bf16[2,128,256]{2,1,0:T(8,128)(2,1)S(1)}, u32[]{:S(2)}, u32[]{:S(2)}) %collective-permute-start.30) | collective-permute-done | bytes 131104 | tf_op jit(solution)/shard_map/ppermute | solution.py:284
  138.6 7.0 %all-to-all-start.3 = ((bf16[8,2,64,256]{3,2,1,0:T(8,128)(2,1)}), bf16[8,2,64,256]{3,2,1,0:T(8,128)(2,1)S(1)}, u32[]{:S(2)}, u32[]{:S(2)}) async-start(bf16[8,2,64,256]{3,2,1,0:T(8,128)(2,1)} %partial_gradient.3), calls=%async_computation.3 | async-start | bytes 1048576 | tf_op jit(solution)/shard_map/all_to_all | solution.py:366
  145.5 15.6 %all-to-all-done.3.refs_0_ = bf16[8,2,64,256]{3,2,1,0:T(8,128)(2,1)S(1)} async-done(((bf16[8,2,64,256]{3,2,1,0:T(8,128)(2,1)}), bf16[8,2,64,256]{3,2,1,0:T(8,128)(2,1)S(1)}, u32[]{:S(2)}, u32[]{:S(2)}) %all-to-all-start.3) | async-done | bytes 524320 | tf_op jit(solution)/shard_map/all_to_all | solution.py:366
  162.0 2.7 %collective-permute-start.34 = (f32[64,256]{1,0:T(8,128)S(1)}, f32[64,256]{1,0:T(8,128)S(1)}, u32[]{:S(2)}, u32[]{:S(2)}) collective-permute-start(f32[64,256]{1,0:T(8,128)S(1)} %get-tuple-element.51), channel_id=1, source_target_pairs={{0,128},{32,160},{128,0},{160,32},{1,129},{33,161},{129,1},{161,33... | collective-permute-start | bytes 196616 | tf_op jit(solution)/shard_map/ppermute | solution.py:289
  169.0 4.4 %collective-permute-start.36 = (f32[64,256]{1,0:T(8,128)S(1)}, f32[64,256]{1,0:T(8,128)S(1)}, u32[]{:S(2)}, u32[]{:S(2)}) collective-permute-start(f32[64,256]{1,0:T(8,128)S(1)} %add_multiply_fusion), channel_id=1, source_target_pairs={{0,64},{64,0},{1,65},{65,1},{2,66},{66,2},{3,67},{67,3},{4,68},{68... | collective-permute-start | bytes 196616 | tf_op jit(solution)/shard_map/ppermute | solution.py:289
  (109 shorter events, 50.0 us)
Async XLA Ops:
  3.0 38.9 %all-to-all-start = ((bf16[16,64,256]{2,1,0:T(8,128)(2,1)}), bf16[16,64,256]{2,1,0:T(8,128)(2,1)S(1)}, u32[]{:S(2)}, u32[]{:S(2)}) async-start(bf16[16,64,256]{2,1,0:T(8,128)(2,1)} %broadcast_in_dim.2), calls=%async_computation | async-start | bytes 1048576 | tf_op jit(solution)/shard_map/all_to_all | solution.py:335
  15.1 20.3 %collective-permute-start = (bf16[128,1024]{1,0:T(8,128)(2,1)S(1)}, bf16[128,1024]{1,0:T(8,128)(2,1)S(1)}, u32[]{:S(2)}, u32[]{:S(2)}) collective-permute-start(bf16[128,1024]{1,0:T(8,128)(2,1)S(1)} %get-tuple-element.22.refs_4_), channel_id=1, source_target_pairs={{0,0},{8,8},{16,16},{24,24},{32,64},{40,72},{48,80},{56,88},{64,32... | collective-permute-start | bytes 786440 | tf_op jit(solution)/shard_map/ppermute | solution.py:315
  19.5 15.9 %collective-permute-start.1 = (bf16[128,1024]{1,0:T(8,128)(2,1)S(1)}, bf16[128,1024]{1,0:T(8,128)(2,1)S(1)}, u32[]{:S(2)}, u32[]{:S(2)}) collective-permute-start(bf16[128,1024]{1,0:T(8,128)(2,1)S(1)} %get-tuple-element.23), channel_id=1, source_target_pairs={{0,8},{8,16},{16,24},{24,0},{32,72},{40,80},{48,88},{56,64},{64,40... | collective-permute-start | bytes 786440 | tf_op jit(solution)/shard_map/ppermute | solution.py:315
  20.6 15.9 %collective-permute-start.2 = (bf16[128,1024]{1,0:T(8,128)(2,1)S(1)}, bf16[128,1024]{1,0:T(8,128)(2,1)S(1)}, u32[]{:S(2)}, u32[]{:S(2)}) collective-permute-start(bf16[128,1024]{1,0:T(8,128)(2,1)S(1)} %get-tuple-element.24), channel_id=1, source_target_pairs={{0,16},{8,24},{16,0},{24,8},{32,80},{40,88},{48,64},{56,72},{64,48... | collective-permute-start | bytes 786440 | tf_op jit(solution)/shard_map/ppermute | solution.py:315
  24.5 12.4 %collective-permute-start.3 = (bf16[128,1024]{1,0:T(8,128)(2,1)S(1)}, bf16[128,1024]{1,0:T(8,128)(2,1)S(1)}, u32[]{:S(2)}, u32[]{:S(2)}) collective-permute-start(bf16[128,1024]{1,0:T(8,128)(2,1)S(1)} %get-tuple-element.25), channel_id=1, source_target_pairs={{0,24},{8,0},{16,8},{24,16},{32,88},{40,64},{48,72},{56,80},{64,56... | collective-permute-start | bytes 786440 | tf_op jit(solution)/shard_map/ppermute | solution.py:315
  37.8 14.0 %collective-permute-start.12 = (f32[2,128,256]{2,1,0:T(8,128)}, f32[2,128,256]{2,1,0:T(8,128)S(1)}, u32[]{:S(2)}, u32[]{:S(2)}) collective-permute-start(f32[2,128,256]{2,1,0:T(8,128)} %get-tuple-element.49), channel_id=1, source_target_pairs={{0,0},{32,64},{64,32},{96,96},{1,1},{33,65},{65,33},{97,97},{2,2},... | collective-permute-start | bytes 786440 | tf_op jit(solution)/shard_map/ppermute | solution.py:326
  41.7 10.0 %collective-permute-start.13 = (f32[2,128,256]{2,1,0:T(8,128)}, f32[2,128,256]{2,1,0:T(8,128)S(1)}, u32[]{:S(2)}, u32[]{:S(2)}) collective-permute-start(f32[2,128,256]{2,1,0:T(8,128)} %get-tuple-element.48), channel_id=1, source_target_pairs={{0,64},{32,0},{64,96},{96,32},{1,65},{33,1},{65,97},{97,33},{2,66}... | collective-permute-start | bytes 786440 | tf_op jit(solution)/shard_map/ppermute | solution.py:327
  42.6 9.2 %collective-permute-start.9 = (bf16[2,128,256]{2,1,0:T(8,128)(2,1)S(1)}, bf16[2,128,256]{2,1,0:T(8,128)(2,1)S(1)}, u32[]{:S(2)}, u32[]{:S(2)}) collective-permute-start(bf16[2,128,256]{2,1,0:T(8,128)(2,1)S(1)} %get-tuple-element.27), channel_id=1, source_target_pairs={{0,24},{8,0},{16,8},{24,16},{1,25},{9,1},{17,9},{25,17},{2,26},{10... | collective-permute-start | bytes 393224 | tf_op jit(solution)/shard_map/ppermute | solution.py:284
  45.7 9.2 %collective-permute-start.11 = (bf16[2,128,256]{2,1,0:T(8,128)(2,1)S(1)}, bf16[2,128,256]{2,1,0:T(8,128)(2,1)S(1)}, u32[]{:S(2)}, u32[]{:S(2)}) collective-permute-start(bf16[2,128,256]{2,1,0:T(8,128)(2,1)S(1)} %get-tuple-element.29), channel_id=1, source_target_pairs={{0,8},{8,16},{16,24},{24,0},{1,9},{9,17},{17,25},{25,1},{2,10},{10... | collective-permute-start | bytes 393224 | tf_op jit(solution)/shard_map/ppermute | solution.py:284
  55.1 9.0 %collective-permute-start.14 = (bf16[2,128,256]{2,1,0:T(8,128)(2,1)S(1)}, bf16[2,128,256]{2,1,0:T(8,128)(2,1)S(1)}, u32[]{:S(2)}, u32[]{:S(2)}) collective-permute-start(bf16[2,128,256]{2,1,0:T(8,128)(2,1)S(1)} %value_gradient.2.refs_8_), channel_id=1, source_target_pairs={{0,8},{8,16},{16,24},{24,0},{1,9},{9,17},{17,25},{25,1},{2,10},{10... | collective-permute-start | bytes 393224 | tf_op jit(solution)/shard_map/ppermute | solution.py:284
  55.2 8.9 %collective-permute-start.15 = (bf16[2,128,256]{2,1,0:T(8,128)(2,1)S(1)}, bf16[2,128,256]{2,1,0:T(8,128)(2,1)S(1)}, u32[]{:S(2)}, u32[]{:S(2)}) collective-permute-start(bf16[2,128,256]{2,1,0:T(8,128)(2,1)S(1)} %value_gradient.2.refs_8_), channel_id=1, source_target_pairs={{0,16},{8,24},{16,0},{24,8},{1,17},{9,25},{17,1},{25,9},{2,18},{10... | collective-permute-start | bytes 393224 | tf_op jit(solution)/shard_map/ppermute | solution.py:284
  65.8 24.9 %all-to-all-start.1 = ((bf16[8,2,64,256]{3,2,1,0:T(8,128)(2,1)}), bf16[8,2,64,256]{3,2,1,0:T(8,128)(2,1)S(1)}, u32[]{:S(2)}, u32[]{:S(2)}) async-start(bf16[8,2,64,256]{3,2,1,0:T(8,128)(2,1)} %partial_gradient.2.refs_2_), calls=%async_computation.1 | async-start | bytes 1048576 | tf_op jit(solution)/shard_map/all_to_all | solution.py:366
  72.1 16.1 %collective-permute-start.8 = (bf16[128,1024]{1,0:T(8,128)(2,1)S(1)}, bf16[128,1024]{1,0:T(8,128)(2,1)S(1)}, u32[]{:S(2)}, u32[]{:S(2)}) collective-permute-start(bf16[128,1024]{1,0:T(8,128)(2,1)S(1)} %slabs.4.refs_7_), channel_id=1, source_target_pairs={{0,0},{8,8},{16,16},{24,24},{32,64},{40,72},{48,80},{56,88},{64,32... | collective-permute-start | bytes 786440 | tf_op jit(solution)/shard_map/ppermute | solution.py:315
  76.1 12.2 %collective-permute-start.25 = (f32[2,128,256]{2,1,0:T(8,128)S(1)}, f32[2,128,256]{2,1,0:T(8,128)S(1)}, u32[]{:S(2)}, u32[]{:S(2)}) collective-permute-start(f32[2,128,256]{2,1,0:T(8,128)S(1)} %get-tuple-element.47), channel_id=1, source_target_pairs={{0,0},{32,64},{64,32},{96,96},{1,1},{33,65},{65,33},{97,97},{2,2},... | collective-permute-start | bytes 786440 | tf_op jit(solution)/shard_map/ppermute | solution.py:326
  78.0 10.3 %collective-permute-start.26 = (f32[2,128,256]{2,1,0:T(8,128)S(1)}, f32[2,128,256]{2,1,0:T(8,128)S(1)}, u32[]{:S(2)}, u32[]{:S(2)}) collective-permute-start(f32[2,128,256]{2,1,0:T(8,128)S(1)} %get-tuple-element.46), channel_id=1, source_target_pairs={{0,64},{32,0},{64,96},{96,32},{1,65},{33,1},{65,97},{97,33},{2,66}... | collective-permute-start | bytes 786440 | tf_op jit(solution)/shard_map/ppermute | solution.py:327
  79.9 10.7 %collective-permute-start.17 = (bf16[128,1024]{1,0:T(8,128)(2,1)S(1)}, bf16[128,1024]{1,0:T(8,128)(2,1)S(1)}, u32[]{:S(2)}, u32[]{:S(2)}) collective-permute-start(bf16[128,1024]{1,0:T(8,128)(2,1)S(1)} %get-tuple-element.30), channel_id=1, source_target_pairs={{0,8},{8,16},{16,24},{24,0},{32,72},{40,80},{48,88},{56,64},{64,40... | collective-permute-start | bytes 786440 | tf_op jit(solution)/shard_map/ppermute | solution.py:315
  91.6 24.2 %all-to-all-start.2 = ((bf16[8,2,64,256]{3,2,1,0:T(8,128)(2,1)}), bf16[8,2,64,256]{3,2,1,0:T(8,128)(2,1)S(1)}, u32[]{:S(2)}, u32[]{:S(2)}) async-start(bf16[8,2,64,256]{3,2,1,0:T(8,128)(2,1)} %get-tuple-element.33), calls=%async_computation.2 | async-start | bytes 1048576 | tf_op jit(solution)/shard_map/all_to_all | solution.py:371
  98.6 10.3 %collective-permute-start.18 = (bf16[128,1024]{1,0:T(8,128)(2,1)S(1)}, bf16[128,1024]{1,0:T(8,128)(2,1)S(1)}, u32[]{:S(2)}, u32[]{:S(2)}) collective-permute-start(bf16[128,1024]{1,0:T(8,128)(2,1)S(1)} %get-tuple-element.31), channel_id=1, source_target_pairs={{0,16},{8,24},{16,0},{24,8},{32,80},{40,88},{48,64},{56,72},{64,48... | collective-permute-start | bytes 786440 | tf_op jit(solution)/shard_map/ppermute | solution.py:315
  99.7 14.1 %collective-permute-start.19 = (bf16[128,1024]{1,0:T(8,128)(2,1)S(1)}, bf16[128,1024]{1,0:T(8,128)(2,1)S(1)}, u32[]{:S(2)}, u32[]{:S(2)}) collective-permute-start(bf16[128,1024]{1,0:T(8,128)(2,1)S(1)} %get-tuple-element.32), channel_id=1, source_target_pairs={{0,24},{8,0},{16,8},{24,16},{32,88},{40,64},{48,72},{56,80},{64,56... | collective-permute-start | bytes 786440 | tf_op jit(solution)/shard_map/ppermute | solution.py:315
  101.3 13.4 %collective-permute-start.20 = (bf16[128,1024]{1,0:T(8,128)(2,1)S(1)}, bf16[128,1024]{1,0:T(8,128)(2,1)S(1)}, u32[]{:S(2)}, u32[]{:S(2)}) collective-permute-start(bf16[128,1024]{1,0:T(8,128)(2,1)S(1)} %collective-permute-done.8.refs_4_.refs_0_), channel_id=1, source_target_pairs={{0,64},{64,0},{1,65},{65,1},{2,66},{66,2},{3,67},{67,3},{4,68},{68... | collective-permute-start | bytes 786440 | tf_op jit(solution)/shard_map/ppermute | solution.py:289
  102.7 11.9 %collective-permute-start.21 = (bf16[128,1024]{1,0:T(8,128)(2,1)S(1)}, bf16[128,1024]{1,0:T(8,128)(2,1)S(1)}, u32[]{:S(2)}, u32[]{:S(2)}) collective-permute-start(bf16[128,1024]{1,0:T(8,128)(2,1)S(1)} %collective-permute-done.17.refs_5_.refs_1_), channel_id=1, source_target_pairs={{0,64},{64,0},{1,65},{65,1},{2,66},{66,2},{3,67},{67,3},{4,68},{68... | collective-permute-start | bytes 786440 | tf_op jit(solution)/shard_map/ppermute | solution.py:289
  118.8 9.1 %collective-permute-start.29 = (bf16[2,128,256]{2,1,0:T(8,128)(2,1)S(1)}, bf16[2,128,256]{2,1,0:T(8,128)(2,1)S(1)}, u32[]{:S(2)}, u32[]{:S(2)}) collective-permute-start(bf16[2,128,256]{2,1,0:T(8,128)(2,1)S(1)} %get-tuple-element.37), channel_id=1, source_target_pairs={{0,8},{8,16},{16,24},{24,0},{1,9},{9,17},{17,25},{25,1},{2,10},{10... | collective-permute-start | bytes 393224 | tf_op jit(solution)/shard_map/ppermute | solution.py:284
  128.2 8.8 %collective-permute-start.30 = (bf16[2,128,256]{2,1,0:T(8,128)(2,1)S(1)}, bf16[2,128,256]{2,1,0:T(8,128)(2,1)S(1)}, u32[]{:S(2)}, u32[]{:S(2)}) collective-permute-start(bf16[2,128,256]{2,1,0:T(8,128)(2,1)S(1)} %value_gradient.3.refs_8_), channel_id=1, source_target_pairs={{0,8},{8,16},{16,24},{24,0},{1,9},{9,17},{17,25},{25,1},{2,10},{10... | collective-permute-start | bytes 393224 | tf_op jit(solution)/shard_map/ppermute | solution.py:284
  138.6 22.5 %all-to-all-start.3 = ((bf16[8,2,64,256]{3,2,1,0:T(8,128)(2,1)}), bf16[8,2,64,256]{3,2,1,0:T(8,128)(2,1)S(1)}, u32[]{:S(2)}, u32[]{:S(2)}) async-start(bf16[8,2,64,256]{3,2,1,0:T(8,128)(2,1)} %partial_gradient.3), calls=%async_computation.3 | async-start | bytes 1048576 | tf_op jit(solution)/shard_map/all_to_all | solution.py:366
  (30 other events, 256.1 us)

commit v3 on v2

--- a/solution.py
+++ b/solution.py
@@ -234,10 +234,12 @@
 
 
 def adam_body(*refs, step, floor, last):
-    if step == 0:
+    if last:
+        recv, theta_ref, m_ref, u_ref, start_ref, place_ref, near, far = refs
+    elif step == 0:
         recv, theta_ref, m_out, u_out, theta_out, sent = refs
     else:
-        recv, theta_ref, m_ref, u_ref, start_ref, m_out, u_out, theta_out, sent = refs
+        recv, theta_ref, m_ref, u_ref, m_out, u_out, theta_out, sent = refs
     gradient = recv[0].astype(F32)
     for z in range(1, recv.shape[0]):
         gradient = gradient + recv[z].astype(F32)
@@ -252,28 +254,35 @@
     theta = theta - inner_rate * (
         corrected_one / (jnp.sqrt(corrected_two) + floor) + decay_rate * theta
     )
+    if last:
+        delta = start_ref[...] - theta
+        swap = place_ref[0] == 1
+        near[...] = jnp.where(swap, delta[1], delta[0])
+        far[...] = jnp.where(swap, delta[0], delta[1])
+        return
     m_out[...] = moment_one
     u_out[...] = moment_two
     theta_out[...] = theta
-    if last:
-        sent[...] = start_ref[...] - theta
-    else:
-        rounded = theta.astype(BF16)
-        for z in range(recv.shape[0]):
-            sent[z] = rounded
+    rounded = theta.astype(BF16)
+    for z in range(recv.shape[0]):
+        sent[z] = rounded
 
 
 def adam(received, state, step, floor, last, after):
     shape = received.shape[1:]
-    sent = shape_of(shape, F32) if last else shape_of(received.shape, BF16)
+    specs = [VMEM_SPEC] * (1 + len(state))
+    outs = [shape_of(shape, F32)] * 3 + [shape_of(received.shape, BF16)]
+    if last:
+        specs[-1] = SMEM_SPEC
+        outs = [shape_of(shape[1:], F32)] * 2
     return pl.pallas_call(
         without(
             lambda *refs: adam_body(*refs, step=step, floor=floor, last=last),
             1 + len(state),
             len(after),
         ),
-        in_specs=[VMEM_SPEC] * (1 + len(state)) + [ANY_SPEC] * len(after),
-        out_shape=[shape_of(shape, F32)] * 3 + [sent],
+        in_specs=specs + [ANY_SPEC] * len(after),
+        out_shape=outs,
         compiler_params=PARAMS,
         name="adam",
     )(received, *state, *after)
@@ -364,15 +373,15 @@
             moved = [swapped(slab, k) for k, slab in enumerate(moved)]
             after = [*sums, *moved[:2]]
         received = lax.all_to_all(scattered, "z", 0, 0, tiled=True)
-        args = (theta,) if step == 0 else (theta, *state, start)
-        m, u, theta, sent = adam(received, args, step, floor, last, after)
-        state = (m, u)
-        if not last:
+        if last:
+            args = (theta, *state, start, y_place)
+            near, far = adam(received, args, step, floor, last, after)
+        else:
+            m, u, theta, sent = adam(received, (theta, *state), step, floor, last, after)
+            state = (m, u)
             gathered = lax.all_to_all(sent, "z", 0, 0, tiled=True)
             slabs = both_cores(moved)
 
-    near = lax.dynamic_index_in_dim(sent, y, 0, False)
-    far = lax.dynamic_index_in_dim(sent, 1 - y, 0, False)
     total = (near + flipped(far, ("yh", "y"), 1)) + (
         flipped(near, ("yh", "y"), 2) + flipped(far, ("yh", "y"), 3)
     )

time: 176 us -> 174 us (0.989)
  blocking collectives: 0 us -> 21.2 us
  waiting for transfers between devices: 67.5 us -> 51.9 us
  starting transfers between devices: 79.5 us -> 73.5 us
    all_to_all x0 -> x1, blocking collectives: none -> 21.2 us  [shards(): received = lax.all_to_all(scattered, 'z', 0, 0, tiled=True)]
    all_to_all x2 -> x1, waiting for transfers between devices: 15.6 us -> 0.01 us  [shards(): received = lax.all_to_all(scattered, 'z', 0, 0, tiled=True)]
    all_to_all x2 -> x1, starting transfers between devices: 13.3 us -> 6.37 us  [shards(): received = lax.all_to_all(scattered, 'z', 0, 0, tiled=True)]
  transfers between devices with their start and end apart: 41 -> 40, of which waited for: 18 -> 17; matrix products, arithmetic and copies ran while one was open for 0% -> 1% of each run, Pallas kernels for 5% -> 5%
where the time goes in v3:
time: 174 us; the launch traced here: 173 us
  starting transfers between devices  73.5 us (42%)
  waiting for transfers between devices  51.9 us (30%)
  blocking collectives  21.2 us (12%)
  Pallas kernels  13.6 us (8%)
  local copies, waits for them, and re-layouts  9.74 us (6%)
  other arithmetic  2.24 us (1%)
    ppermute x12, waiting for transfers between devices, shifted(): return lax.ppermute(value, axis, [(i, (i + k) % size) for i in range(size)])  23.8 us
    all_to_all x1, blocking collectives, shards(): received = lax.all_to_all(scattered, 'z', 0, 0, tiled=True)  21.2 us
    ppermute x8, starting transfers between devices, swapped(): return lax.ppermute(slab, ('c', 'y', 'x'), pairs)  18.3 us
    ppermute x8, waiting for transfers between devices, swapped(): return lax.ppermute(slab, ('c', 'y', 'x'), pairs)  16 us
    ppermute x13, starting transfers between devices, flipped(): return lax.ppermute(value, axis, [(i, i ^ mask) for i in range(size)])  13.6 us
    ppermute x13, waiting for transfers between devices, flipped(): return lax.ppermute(value, axis, [(i, i ^ mask) for i in range(size)])  12.1 us
    ppermute x12, starting transfers between devices, shifted(): return lax.ppermute(value, axis, [(i, (i + k) % size) for i in range(size)])  12.1 us
    all_to_all x1, starting transfers between devices, shards(): lax.all_to_all(jnp.broadcast_to(first[None], (zs * ys, *first.shape)), ('...  10.3 us
  transfers between devices with their start and end apart: 40, of which 17 were waited for; matrix products, arithmetic and copies ran while one was open for 1% of the time, Pallas kernels for 5%

profile of v3, /device:TPU:1, one launch (start us, length us, event | category | flops | bytes accessed | tf_op | source)
XLA Modules:
  0.0 173.3 jit_solution(18034418775233108317)
XLA Ops:
  3.0 10.3 %all-to-all-start = ((bf16[16,64,256]{2,1,0:T(8,128)(2,1)}), bf16[16,64,256]{2,1,0:T(8,128)(2,1)S(1)}, u32[]{:S(2)}, u32[]{:S(2)}) async-start(bf16[16,64,256]{2,1,0:T(8,128)(2,1)} %broadcast_in_dim.2), calls=%async_computation | async-start | bytes 1048576 | tf_op jit(solution)/shard_map/all_to_all | solution.py:344
  15.2 4.4 %collective-permute-start = (bf16[128,1024]{1,0:T(8,128)(2,1)S(1)}, bf16[128,1024]{1,0:T(8,128)(2,1)S(1)}, u32[]{:S(2)}, u32[]{:S(2)}) collective-permute-start(bf16[128,1024]{1,0:T(8,128)(2,1)S(1)} %get-tuple-element.23.refs_4_), channel_id=1, source_target_pairs={{0,0},{8,8},{16,16},{24,24},{32,64},{40,72},{48,80},{56,88},{64,32... | collective-permute-start | bytes 786440 | tf_op jit(solution)/shard_map/ppermute | solution.py:324
  20.6 3.9 %collective-permute-start.2 = (bf16[128,1024]{1,0:T(8,128)(2,1)S(1)}, bf16[128,1024]{1,0:T(8,128)(2,1)S(1)}, u32[]{:S(2)}, u32[]{:S(2)}) collective-permute-start(bf16[128,1024]{1,0:T(8,128)(2,1)S(1)} %get-tuple-element.25), channel_id=1, source_target_pairs={{0,16},{8,24},{16,0},{24,8},{32,80},{40,88},{48,64},{56,72},{64,48... | collective-permute-start | bytes 786440 | tf_op jit(solution)/shard_map/ppermute | solution.py:324
  28.5 3.8 %attention_sums.2.after_ref = f32[4,128,256]{2,1,0:T(8,128)S(1)} custom-call(s32[1]{0:T(128)} %bitcast.1.refs_0_.refs_5_, bf16[2,128,4096]{2,1,0:T(8,128)(2,1)S(1)} %copy-done.2, bf16[2,128,512]{2,1,0:T(8,128)(2,1)S(1)} %copy-done.9, bf16[2,128,4096]{2,1,0:T(8,128)(2,1)S(1)} %copy-done.4, bf16[128,1024]{1,0:T(8,128)(2,1)S(1)} %get-tuple-element.23.refs_4_), custom_call_target="tpu_custom_call" | custom-call | flops 2147483648 | bytes 1024 | tf_op jit(solution)/shard_map/attention_sums/pallas_call | solution.py:91
  32.3 3.2 %collective-permute-done.value_ref = bf16[128,1024]{1,0:T(8,128)(2,1)S(1)} collective-permute-done((bf16[128,1024]{1,0:T(8,128)(2,1)S(1)}, bf16[128,1024]{1,0:T(8,128)(2,1)S(1)}, u32[]{:S(2)}, u32[]{:S(2)}) %collective-permute-start) | collective-permute-done | bytes 262176 | tf_op jit(solution)/shard_map/ppermute | solution.py:324
  37.8 3.9 %collective-permute-start.12 = (f32[2,128,256]{2,1,0:T(8,128)}, f32[2,128,256]{2,1,0:T(8,128)S(1)}, u32[]{:S(2)}, u32[]{:S(2)}) collective-permute-start(f32[2,128,256]{2,1,0:T(8,128)} %get-tuple-element.51), channel_id=1, source_target_pairs={{0,0},{32,64},{64,32},{96,96},{1,1},{33,65},{65,33},{97,97},{2,2},... | collective-permute-start | bytes 786440 | tf_op jit(solution)/shard_map/ppermute | solution.py:335
  42.6 2.6 %collective-permute-start.9 = (bf16[2,128,256]{2,1,0:T(8,128)(2,1)S(1)}, bf16[2,128,256]{2,1,0:T(8,128)(2,1)S(1)}, u32[]{:S(2)}, u32[]{:S(2)}) collective-permute-start(bf16[2,128,256]{2,1,0:T(8,128)(2,1)S(1)} %get-tuple-element.28), channel_id=1, source_target_pairs={{0,24},{8,0},{16,8},{24,16},{1,25},{9,1},{17,9},{25,17},{2,26},{10... | collective-permute-start | bytes 393224 | tf_op jit(solution)/shard_map/ppermute | solution.py:293
  47.9 3.8 %attention_sums.3.refs_6_ = f32[4,128,256]{2,1,0:T(8,128)S(1)} custom-call(s32[1]{0:T(128)} %bitcast.1.refs_0_.refs_5_, bf16[2,128,4096]{2,1,0:T(8,128)(2,1)S(1)} %copy-done.3, bf16[2,128,512]{2,1,0:T(8,128)(2,1)S(1)} %copy-done.9, bf16[2,128,4096]{2,1,0:T(8,128)(2,1)S(1)} %copy-done.5, f32[2,128,256]{2,1,0:T(8,128)S(1)} %get-tuple-element.27.refs_2_.refs_4_.refs_0_), custom_call_target="tpu_custom_call" | custom-call | flops 2147483648 | bytes 1024 | tf_op jit(solution)/shard_map/attention_sums/pallas_call | solution.py:91
  51.8 3.1 %collective-permute-done.11.refs_3_ = bf16[2,128,256]{2,1,0:T(8,128)(2,1)S(1)} collective-permute-done((bf16[2,128,256]{2,1,0:T(8,128)(2,1)S(1)}, bf16[2,128,256]{2,1,0:T(8,128)(2,1)S(1)}, u32[]{:S(2)}, u32[]{:S(2)}) %collective-permute-start.11) | collective-permute-done | bytes 131104 | tf_op jit(solution)/shard_map/ppermute | solution.py:293
  57.9 6.2 %collective-permute-done.14.refs_9_ = bf16[2,128,256]{2,1,0:T(8,128)(2,1)S(1)} collective-permute-done((bf16[2,128,256]{2,1,0:T(8,128)(2,1)S(1)}, bf16[2,128,256]{2,1,0:T(8,128)(2,1)S(1)}, u32[]{:S(2)}, u32[]{:S(2)}) %collective-permute-start.14) | collective-permute-done | bytes 131104 | tf_op jit(solution)/shard_map/ppermute | solution.py:293
  65.8 6.4 %all-to-all-start.1 = ((bf16[8,2,64,256]{3,2,1,0:T(8,128)(2,1)}), bf16[8,2,64,256]{3,2,1,0:T(8,128)(2,1)S(1)}, u32[]{:S(2)}, u32[]{:S(2)}) async-start(bf16[8,2,64,256]{3,2,1,0:T(8,128)(2,1)} %partial_gradient.2.refs_2_), calls=%async_computation.1 | async-start | bytes 1048576 | tf_op jit(solution)/shard_map/all_to_all | solution.py:375
  72.2 3.9 %collective-permute-start.8 = (bf16[128,1024]{1,0:T(8,128)(2,1)S(1)}, bf16[128,1024]{1,0:T(8,128)(2,1)S(1)}, u32[]{:S(2)}, u32[]{:S(2)}) collective-permute-start(bf16[128,1024]{1,0:T(8,128)(2,1)S(1)} %slabs.4.refs_7_), channel_id=1, source_target_pairs={{0,0},{8,8},{16,16},{24,24},{32,64},{40,72},{48,80},{56,88},{64,32... | collective-permute-start | bytes 786440 | tf_op jit(solution)/shard_map/ppermute | solution.py:324
  82.0 6.3 %collective-permute-done.24 = f32[64,256]{1,0:T(8,128)S(1)} collective-permute-done((f32[64,256]{1,0:T(8,128)S(1)}, f32[64,256]{1,0:T(8,128)S(1)}, u32[]{:S(2)}, u32[]{:S(2)}) %collective-permute-start.24) | collective-permute-done | bytes 65568 | tf_op jit(solution)/shard_map/ppermute | solution.py:298
  88.3 2.3 %collective-permute-done.17.refs_5_.refs_1_ = bf16[128,1024]{1,0:T(8,128)(2,1)S(1)} collective-permute-done((bf16[128,1024]{1,0:T(8,128)(2,1)S(1)}, bf16[128,1024]{1,0:T(8,128)(2,1)S(1)}, u32[]{:S(2)}, u32[]{:S(2)}) %collective-permute-start.17) | collective-permute-done | bytes 262176 | tf_op jit(solution)/shard_map/ppermute | solution.py:324
  91.7 6.9 %all-to-all-start.2 = ((bf16[8,2,64,256]{3,2,1,0:T(8,128)(2,1)}), bf16[8,2,64,256]{3,2,1,0:T(8,128)(2,1)S(1)}, u32[]{:S(2)}, u32[]{:S(2)}) async-start(bf16[8,2,64,256]{3,2,1,0:T(8,128)(2,1)} %get-tuple-element.34), calls=%async_computation.2 | async-start | bytes 1048576 | tf_op jit(solution)/shard_map/all_to_all | solution.py:382
  102.8 6.1 %collective-permute-done.18.refs_2_ = bf16[128,1024]{1,0:T(8,128)(2,1)S(1)} collective-permute-done((bf16[128,1024]{1,0:T(8,128)(2,1)S(1)}, bf16[128,1024]{1,0:T(8,128)(2,1)S(1)}, u32[]{:S(2)}, u32[]{:S(2)}) %collective-permute-start.18) | collective-permute-done | bytes 262176 | tf_op jit(solution)/shard_map/ppermute | solution.py:324
  110.2 3.5 %collective-permute-done.19.refs_3_ = bf16[128,1024]{1,0:T(8,128)(2,1)S(1)} collective-permute-done((bf16[128,1024]{1,0:T(8,128)(2,1)S(1)}, bf16[128,1024]{1,0:T(8,128)(2,1)S(1)}, u32[]{:S(2)}, u32[]{:S(2)}) %collective-permute-start.19) | collective-permute-done | bytes 262176 | tf_op jit(solution)/shard_map/ppermute | solution.py:324
  119.5 4.8 %collective-permute-done.27.refs_1_ = bf16[2,128,256]{2,1,0:T(8,128)(2,1)S(1)} collective-permute-done((bf16[2,128,256]{2,1,0:T(8,128)(2,1)S(1)}, bf16[2,128,256]{2,1,0:T(8,128)(2,1)S(1)}, u32[]{:S(2)}, u32[]{:S(2)}) %collective-permute-start.27) | collective-permute-done | bytes 131104 | tf_op jit(solution)/shard_map/ppermute | solution.py:293
  124.8 3.2 %collective-permute-done.29.refs_3_ = bf16[2,128,256]{2,1,0:T(8,128)(2,1)S(1)} collective-permute-done((bf16[2,128,256]{2,1,0:T(8,128)(2,1)S(1)}, bf16[2,128,256]{2,1,0:T(8,128)(2,1)S(1)}, u32[]{:S(2)}, u32[]{:S(2)}) %collective-permute-start.29) | collective-permute-done | bytes 131104 | tf_op jit(solution)/shard_map/ppermute | solution.py:293
  131.0 6.0 %collective-permute-done.30.refs_9_ = bf16[2,128,256]{2,1,0:T(8,128)(2,1)S(1)} collective-permute-done((bf16[2,128,256]{2,1,0:T(8,128)(2,1)S(1)}, bf16[2,128,256]{2,1,0:T(8,128)(2,1)S(1)}, u32[]{:S(2)}, u32[]{:S(2)}) %collective-permute-start.30) | collective-permute-done | bytes 131104 | tf_op jit(solution)/shard_map/ppermute | solution.py:293
  137.8 21.2 %all_to_all.20.refs_0_ = bf16[8,2,64,256]{3,2,1,0:T(8,128)(2,1)S(1)} all-to-all(bf16[8,2,64,256]{3,2,1,0:T(8,128)(2,1)S(1)} %partial_gradient.3), channel_id=1, replica_groups=mesh['yh'=2,'c'=2,'y'=2,'x'=4,'z'=8] {'z'}, dimensions={0} | all-to-all | bytes 1048576 | tf_op jit(solution)/shard_map/all_to_all | solution.py:375
  159.2 2.7 %collective-permute-start.34 = (f32[64,256]{1,0:T(8,128)S(1)}, f32[64,256]{1,0:T(8,128)S(1)}, u32[]{:S(2)}, u32[]{:S(2)}) collective-permute-start(f32[64,256]{1,0:T(8,128)S(1)} %get-tuple-element.42), channel_id=1, source_target_pairs={{0,128},{32,160},{128,0},{160,32},{1,129},{33,161},{129,1},{161,33... | collective-permute-start | bytes 196616 | tf_op jit(solution)/shard_map/ppermute | solution.py:298
  163.9 2.3 %collective-permute-done.35 = f32[64,256]{1,0:T(8,128)S(1)} collective-permute-done((f32[64,256]{1,0:T(8,128)S(1)}, f32[64,256]{1,0:T(8,128)S(1)}, u32[]{:S(2)}, u32[]{:S(2)}) %collective-permute-start.35) | collective-permute-done | bytes 65568 | tf_op jit(solution)/shard_map/ppermute | solution.py:298
  166.3 5.4 %collective-permute-start.36 = (f32[64,256]{1,0:T(8,128)S(1)}, f32[64,256]{1,0:T(8,128)S(1)}, u32[]{:S(2)}, u32[]{:S(2)}) collective-permute-start(f32[64,256]{1,0:T(8,128)S(1)} %add_multiply_fusion), channel_id=1, source_target_pairs={{0,64},{64,0},{1,65},{65,1},{2,66},{66,2},{3,67},{67,3},{4,68},{68... | collective-permute-start | bytes 196616 | tf_op jit(solution)/shard_map/ppermute | solution.py:298
  (107 shorter events, 46.2 us)
Async XLA Ops:
  3.0 38.9 %all-to-all-start = ((bf16[16,64,256]{2,1,0:T(8,128)(2,1)}), bf16[16,64,256]{2,1,0:T(8,128)(2,1)S(1)}, u32[]{:S(2)}, u32[]{:S(2)}) async-start(bf16[16,64,256]{2,1,0:T(8,128)(2,1)} %broadcast_in_dim.2), calls=%async_computation | async-start | bytes 1048576 | tf_op jit(solution)/shard_map/all_to_all | solution.py:344
  15.2 20.3 %collective-permute-start = (bf16[128,1024]{1,0:T(8,128)(2,1)S(1)}, bf16[128,1024]{1,0:T(8,128)(2,1)S(1)}, u32[]{:S(2)}, u32[]{:S(2)}) collective-permute-start(bf16[128,1024]{1,0:T(8,128)(2,1)S(1)} %get-tuple-element.23.refs_4_), channel_id=1, source_target_pairs={{0,0},{8,8},{16,16},{24,24},{32,64},{40,72},{48,80},{56,88},{64,32... | collective-permute-start | bytes 786440 | tf_op jit(solution)/shard_map/ppermute | solution.py:324
  19.5 15.9 %collective-permute-start.1 = (bf16[128,1024]{1,0:T(8,128)(2,1)S(1)}, bf16[128,1024]{1,0:T(8,128)(2,1)S(1)}, u32[]{:S(2)}, u32[]{:S(2)}) collective-permute-start(bf16[128,1024]{1,0:T(8,128)(2,1)S(1)} %get-tuple-element.24), channel_id=1, source_target_pairs={{0,8},{8,16},{16,24},{24,0},{32,72},{40,80},{48,88},{56,64},{64,40... | collective-permute-start | bytes 786440 | tf_op jit(solution)/shard_map/ppermute | solution.py:324
  20.6 15.9 %collective-permute-start.2 = (bf16[128,1024]{1,0:T(8,128)(2,1)S(1)}, bf16[128,1024]{1,0:T(8,128)(2,1)S(1)}, u32[]{:S(2)}, u32[]{:S(2)}) collective-permute-start(bf16[128,1024]{1,0:T(8,128)(2,1)S(1)} %get-tuple-element.25), channel_id=1, source_target_pairs={{0,16},{8,24},{16,0},{24,8},{32,80},{40,88},{48,64},{56,72},{64,48... | collective-permute-start | bytes 786440 | tf_op jit(solution)/shard_map/ppermute | solution.py:324
  24.5 12.4 %collective-permute-start.3 = (bf16[128,1024]{1,0:T(8,128)(2,1)S(1)}, bf16[128,1024]{1,0:T(8,128)(2,1)S(1)}, u32[]{:S(2)}, u32[]{:S(2)}) collective-permute-start(bf16[128,1024]{1,0:T(8,128)(2,1)S(1)} %get-tuple-element.26), channel_id=1, source_target_pairs={{0,24},{8,0},{16,8},{24,16},{32,88},{40,64},{48,72},{56,80},{64,56... | collective-permute-start | bytes 786440 | tf_op jit(solution)/shard_map/ppermute | solution.py:324
  37.8 14.0 %collective-permute-start.12 = (f32[2,128,256]{2,1,0:T(8,128)}, f32[2,128,256]{2,1,0:T(8,128)S(1)}, u32[]{:S(2)}, u32[]{:S(2)}) collective-permute-start(f32[2,128,256]{2,1,0:T(8,128)} %get-tuple-element.51), channel_id=1, source_target_pairs={{0,0},{32,64},{64,32},{96,96},{1,1},{33,65},{65,33},{97,97},{2,2},... | collective-permute-start | bytes 786440 | tf_op jit(solution)/shard_map/ppermute | solution.py:335
  41.7 10.0 %collective-permute-start.13 = (f32[2,128,256]{2,1,0:T(8,128)}, f32[2,128,256]{2,1,0:T(8,128)S(1)}, u32[]{:S(2)}, u32[]{:S(2)}) collective-permute-start(f32[2,128,256]{2,1,0:T(8,128)} %get-tuple-element.50), channel_id=1, source_target_pairs={{0,64},{32,0},{64,96},{96,32},{1,65},{33,1},{65,97},{97,33},{2,66}... | collective-permute-start | bytes 786440 | tf_op jit(solution)/shard_map/ppermute | solution.py:336
  42.6 9.2 %collective-permute-start.9 = (bf16[2,128,256]{2,1,0:T(8,128)(2,1)S(1)}, bf16[2,128,256]{2,1,0:T(8,128)(2,1)S(1)}, u32[]{:S(2)}, u32[]{:S(2)}) collective-permute-start(bf16[2,128,256]{2,1,0:T(8,128)(2,1)S(1)} %get-tuple-element.28), channel_id=1, source_target_pairs={{0,24},{8,0},{16,8},{24,16},{1,25},{9,1},{17,9},{25,17},{2,26},{10... | collective-permute-start | bytes 393224 | tf_op jit(solution)/shard_map/ppermute | solution.py:293
  45.7 9.2 %collective-permute-start.11 = (bf16[2,128,256]{2,1,0:T(8,128)(2,1)S(1)}, bf16[2,128,256]{2,1,0:T(8,128)(2,1)S(1)}, u32[]{:S(2)}, u32[]{:S(2)}) collective-permute-start(bf16[2,128,256]{2,1,0:T(8,128)(2,1)S(1)} %get-tuple-element.30), channel_id=1, source_target_pairs={{0,8},{8,16},{16,24},{24,0},{1,9},{9,17},{17,25},{25,1},{2,10},{10... | collective-permute-start | bytes 393224 | tf_op jit(solution)/shard_map/ppermute | solution.py:293
  55.2 9.0 %collective-permute-start.14 = (bf16[2,128,256]{2,1,0:T(8,128)(2,1)S(1)}, bf16[2,128,256]{2,1,0:T(8,128)(2,1)S(1)}, u32[]{:S(2)}, u32[]{:S(2)}) collective-permute-start(bf16[2,128,256]{2,1,0:T(8,128)(2,1)S(1)} %value_gradient.2.refs_8_), channel_id=1, source_target_pairs={{0,8},{8,16},{16,24},{24,0},{1,9},{9,17},{17,25},{25,1},{2,10},{10... | collective-permute-start | bytes 393224 | tf_op jit(solution)/shard_map/ppermute | solution.py:293
  55.3 8.9 %collective-permute-start.15 = (bf16[2,128,256]{2,1,0:T(8,128)(2,1)S(1)}, bf16[2,128,256]{2,1,0:T(8,128)(2,1)S(1)}, u32[]{:S(2)}, u32[]{:S(2)}) collective-permute-start(bf16[2,128,256]{2,1,0:T(8,128)(2,1)S(1)} %value_gradient.2.refs_8_), channel_id=1, source_target_pairs={{0,16},{8,24},{16,0},{24,8},{1,17},{9,25},{17,1},{25,9},{2,18},{10... | collective-permute-start | bytes 393224 | tf_op jit(solution)/shard_map/ppermute | solution.py:293
  65.8 24.9 %all-to-all-start.1 = ((bf16[8,2,64,256]{3,2,1,0:T(8,128)(2,1)}), bf16[8,2,64,256]{3,2,1,0:T(8,128)(2,1)S(1)}, u32[]{:S(2)}, u32[]{:S(2)}) async-start(bf16[8,2,64,256]{3,2,1,0:T(8,128)(2,1)} %partial_gradient.2.refs_2_), calls=%async_computation.1 | async-start | bytes 1048576 | tf_op jit(solution)/shard_map/all_to_all | solution.py:375
  72.2 16.1 %collective-permute-start.8 = (bf16[128,1024]{1,0:T(8,128)(2,1)S(1)}, bf16[128,1024]{1,0:T(8,128)(2,1)S(1)}, u32[]{:S(2)}, u32[]{:S(2)}) collective-permute-start(bf16[128,1024]{1,0:T(8,128)(2,1)S(1)} %slabs.4.refs_7_), channel_id=1, source_target_pairs={{0,0},{8,8},{16,16},{24,24},{32,64},{40,72},{48,80},{56,88},{64,32... | collective-permute-start | bytes 786440 | tf_op jit(solution)/shard_map/ppermute | solution.py:324
  76.1 12.2 %collective-permute-start.25 = (f32[2,128,256]{2,1,0:T(8,128)S(1)}, f32[2,128,256]{2,1,0:T(8,128)S(1)}, u32[]{:S(2)}, u32[]{:S(2)}) collective-permute-start(f32[2,128,256]{2,1,0:T(8,128)S(1)} %get-tuple-element.49), channel_id=1, source_target_pairs={{0,0},{32,64},{64,32},{96,96},{1,1},{33,65},{65,33},{97,97},{2,2},... | collective-permute-start | bytes 786440 | tf_op jit(solution)/shard_map/ppermute | solution.py:335
  78.0 10.3 %collective-permute-start.26 = (f32[2,128,256]{2,1,0:T(8,128)S(1)}, f32[2,128,256]{2,1,0:T(8,128)S(1)}, u32[]{:S(2)}, u32[]{:S(2)}) collective-permute-start(f32[2,128,256]{2,1,0:T(8,128)S(1)} %get-tuple-element.48), channel_id=1, source_target_pairs={{0,64},{32,0},{64,96},{96,32},{1,65},{33,1},{65,97},{97,33},{2,66}... | collective-permute-start | bytes 786440 | tf_op jit(solution)/shard_map/ppermute | solution.py:336
  79.9 10.7 %collective-permute-start.17 = (bf16[128,1024]{1,0:T(8,128)(2,1)S(1)}, bf16[128,1024]{1,0:T(8,128)(2,1)S(1)}, u32[]{:S(2)}, u32[]{:S(2)}) collective-permute-start(bf16[128,1024]{1,0:T(8,128)(2,1)S(1)} %get-tuple-element.31), channel_id=1, source_target_pairs={{0,8},{8,16},{16,24},{24,0},{32,72},{40,80},{48,88},{56,64},{64,40... | collective-permute-start | bytes 786440 | tf_op jit(solution)/shard_map/ppermute | solution.py:324
  91.7 24.2 %all-to-all-start.2 = ((bf16[8,2,64,256]{3,2,1,0:T(8,128)(2,1)}), bf16[8,2,64,256]{3,2,1,0:T(8,128)(2,1)S(1)}, u32[]{:S(2)}, u32[]{:S(2)}) async-start(bf16[8,2,64,256]{3,2,1,0:T(8,128)(2,1)} %get-tuple-element.34), calls=%async_computation.2 | async-start | bytes 1048576 | tf_op jit(solution)/shard_map/all_to_all | solution.py:382
  98.6 10.3 %collective-permute-start.18 = (bf16[128,1024]{1,0:T(8,128)(2,1)S(1)}, bf16[128,1024]{1,0:T(8,128)(2,1)S(1)}, u32[]{:S(2)}, u32[]{:S(2)}) collective-permute-start(bf16[128,1024]{1,0:T(8,128)(2,1)S(1)} %get-tuple-element.32), channel_id=1, source_target_pairs={{0,16},{8,24},{16,0},{24,8},{32,80},{40,88},{48,64},{56,72},{64,48... | collective-permute-start | bytes 786440 | tf_op jit(solution)/shard_map/ppermute | solution.py:324
  99.7 14.1 %collective-permute-start.19 = (bf16[128,1024]{1,0:T(8,128)(2,1)S(1)}, bf16[128,1024]{1,0:T(8,128)(2,1)S(1)}, u32[]{:S(2)}, u32[]{:S(2)}) collective-permute-start(bf16[128,1024]{1,0:T(8,128)(2,1)S(1)} %get-tuple-element.33), channel_id=1, source_target_pairs={{0,24},{8,0},{16,8},{24,16},{32,88},{40,64},{48,72},{56,80},{64,56... | collective-permute-start | bytes 786440 | tf_op jit(solution)/shard_map/ppermute | solution.py:324
  101.3 13.4 %collective-permute-start.20 = (bf16[128,1024]{1,0:T(8,128)(2,1)S(1)}, bf16[128,1024]{1,0:T(8,128)(2,1)S(1)}, u32[]{:S(2)}, u32[]{:S(2)}) collective-permute-start(bf16[128,1024]{1,0:T(8,128)(2,1)S(1)} %collective-permute-done.8.refs_4_.refs_0_), channel_id=1, source_target_pairs={{0,64},{64,0},{1,65},{65,1},{2,66},{66,2},{3,67},{67,3},{4,68},{68... | collective-permute-start | bytes 786440 | tf_op jit(solution)/shard_map/ppermute | solution.py:298
  102.8 11.9 %collective-permute-start.21 = (bf16[128,1024]{1,0:T(8,128)(2,1)S(1)}, bf16[128,1024]{1,0:T(8,128)(2,1)S(1)}, u32[]{:S(2)}, u32[]{:S(2)}) collective-permute-start(bf16[128,1024]{1,0:T(8,128)(2,1)S(1)} %collective-permute-done.17.refs_5_.refs_1_), channel_id=1, source_target_pairs={{0,64},{64,0},{1,65},{65,1},{2,66},{66,2},{3,67},{67,3},{4,68},{68... | collective-permute-start | bytes 786440 | tf_op jit(solution)/shard_map/ppermute | solution.py:298
  118.8 9.1 %collective-permute-start.29 = (bf16[2,128,256]{2,1,0:T(8,128)(2,1)S(1)}, bf16[2,128,256]{2,1,0:T(8,128)(2,1)S(1)}, u32[]{:S(2)}, u32[]{:S(2)}) collective-permute-start(bf16[2,128,256]{2,1,0:T(8,128)(2,1)S(1)} %get-tuple-element.38), channel_id=1, source_target_pairs={{0,8},{8,16},{16,24},{24,0},{1,9},{9,17},{17,25},{25,1},{2,10},{10... | collective-permute-start | bytes 393224 | tf_op jit(solution)/shard_map/ppermute | solution.py:293
  128.3 8.8 %collective-permute-start.30 = (bf16[2,128,256]{2,1,0:T(8,128)(2,1)S(1)}, bf16[2,128,256]{2,1,0:T(8,128)(2,1)S(1)}, u32[]{:S(2)}, u32[]{:S(2)}) collective-permute-start(bf16[2,128,256]{2,1,0:T(8,128)(2,1)S(1)} %value_gradient.3.refs_8_), channel_id=1, source_target_pairs={{0,8},{8,16},{16,24},{24,0},{1,9},{9,17},{17,25},{25,1},{2,10},{10... | collective-permute-start | bytes 393224 | tf_op jit(solution)/shard_map/ppermute | solution.py:293
  128.3 8.7 %collective-permute-start.31 = (bf16[2,128,256]{2,1,0:T(8,128)(2,1)S(1)}, bf16[2,128,256]{2,1,0:T(8,128)(2,1)S(1)}, u32[]{:S(2)}, u32[]{:S(2)}) collective-permute-start(bf16[2,128,256]{2,1,0:T(8,128)(2,1)S(1)} %value_gradient.3.refs_8_), channel_id=1, source_target_pairs={{0,16},{8,24},{16,0},{24,8},{1,17},{9,25},{17,1},{25,9},{2,18},{10... | collective-permute-start | bytes 393224 | tf_op jit(solution)/shard_map/ppermute | solution.py:293
  (29 other events, 263.5 us)

commit v4 on v3

--- a/solution.py
+++ b/solution.py
@@ -371,7 +371,7 @@
             sums = sums_of(later)
             moved += slabs_of(x_place, layer_input, step + 1, ys, xs, every[1:], [scattered])
             moved = [swapped(slab, k) for k, slab in enumerate(moved)]
-            after = [*sums, *moved[:2]]
+            after = [*sums, moved[0]]
         received = lax.all_to_all(scattered, "z", 0, 0, tiled=True)
         if last:
             args = (theta, *state, start, y_place)

time: 174 us -> 174 us (level)
    ppermute x8, waiting for transfers between devices: 16 us -> 14.2 us  [swapped(): return lax.ppermute(slab, ('c', 'y', 'x'), pairs)]
  transfers between devices with their start and end apart: 40 -> 40, of which waited for: 17 -> 19; matrix products, arithmetic and copies ran while one was open for 1% -> 1% of each run, Pallas kernels for 5% -> 5%
where the time goes in v4:
time: 174 us
  starting transfers between devices  72.9 us (42%)
  waiting for transfers between devices  52 us (30%)
  blocking collectives  21.4 us (12%)
  Pallas kernels  13.6 us (8%)
  local copies, waits for them, and re-layouts  10.4 us (6%)
  other arithmetic  2.24 us (1%)
    ppermute x12, waiting for transfers between devices, shifted(): return lax.ppermute(value, axis, [(i, (i + k) % size) for i in range(size)])  24.1 us
    all_to_all x1, blocking collectives, shards(): received = lax.all_to_all(scattered, 'z', 0, 0, tiled=True)  21.4 us
    ppermute x8, starting transfers between devices, swapped(): return lax.ppermute(slab, ('c', 'y', 'x'), pairs)  19.5 us
    ppermute x13, starting transfers between devices, flipped(): return lax.ppermute(value, axis, [(i, i ^ mask) for i in range(size)])  14.4 us
    ppermute x8, waiting for transfers between devices, swapped(): return lax.ppermute(slab, ('c', 'y', 'x'), pairs)  14.2 us
    ppermute x13, waiting for transfers between devices, flipped(): return lax.ppermute(value, axis, [(i, i ^ mask) for i in range(size)])  12.1 us
    ppermute x12, starting transfers between devices, shifted(): return lax.ppermute(value, axis, [(i, (i + k) % size) for i in range(size)])  11 us
    all_to_all x1, starting transfers between devices, shards(): lax.all_to_all(jnp.broadcast_to(first[None], (zs * ys, *first.shape)), ('...  10.3 us
  transfers between devices with their start and end apart: 40, of which 19 were waited for; matrix products, arithmetic and copies ran while one was open for 1% of the time, Pallas kernels for 5%

profile of v4, /device:TPU:1, one launch (start us, length us, event | category | flops | bytes accessed | tf_op | source)
XLA Modules:
  0.0 173.5 jit_solution(7627287709619936120)
XLA Ops:
  3.0 10.3 %all-to-all-start = ((bf16[16,64,256]{2,1,0:T(8,128)(2,1)}), bf16[16,64,256]{2,1,0:T(8,128)(2,1)S(1)}, u32[]{:S(2)}, u32[]{:S(2)}) async-start(bf16[16,64,256]{2,1,0:T(8,128)(2,1)} %broadcast_in_dim.2), calls=%async_computation | async-start | bytes 1048576 | tf_op jit(solution)/shard_map/all_to_all | solution.py:344
  15.2 4.4 %collective-permute-start = (bf16[128,1024]{1,0:T(8,128)(2,1)S(1)}, bf16[128,1024]{1,0:T(8,128)(2,1)S(1)}, u32[]{:S(2)}, u32[]{:S(2)}) collective-permute-start(bf16[128,1024]{1,0:T(8,128)(2,1)S(1)} %get-tuple-element.23.refs_4_), channel_id=1, source_target_pairs={{0,0},{8,8},{16,16},{24,24},{32,64},{40,72},{48,80},{56,88},{64,32... | collective-permute-start | bytes 786440 | tf_op jit(solution)/shard_map/ppermute | solution.py:324
  20.6 3.9 %collective-permute-start.2 = (bf16[128,1024]{1,0:T(8,128)(2,1)S(1)}, bf16[128,1024]{1,0:T(8,128)(2,1)S(1)}, u32[]{:S(2)}, u32[]{:S(2)}) collective-permute-start(bf16[128,1024]{1,0:T(8,128)(2,1)S(1)} %get-tuple-element.25), channel_id=1, source_target_pairs={{0,16},{8,24},{16,0},{24,8},{32,80},{40,88},{48,64},{56,72},{64,48... | collective-permute-start | bytes 786440 | tf_op jit(solution)/shard_map/ppermute | solution.py:324
  28.5 3.8 %attention_sums.2.after_ref = f32[4,128,256]{2,1,0:T(8,128)S(1)} custom-call(s32[1]{0:T(128)} %bitcast.1.refs_0_.refs_5_, bf16[2,128,4096]{2,1,0:T(8,128)(2,1)S(1)} %copy-done.2, bf16[2,128,512]{2,1,0:T(8,128)(2,1)S(1)} %copy-done.9, bf16[2,128,4096]{2,1,0:T(8,128)(2,1)S(1)} %copy-done.4, bf16[128,1024]{1,0:T(8,128)(2,1)S(1)} %get-tuple-element.23.refs_4_), custom_call_target="tpu_custom_call" | custom-call | flops 2147483648 | bytes 1024 | tf_op jit(solution)/shard_map/attention_sums/pallas_call | solution.py:91
  32.3 3.2 %collective-permute-done.value_ref = bf16[128,1024]{1,0:T(8,128)(2,1)S(1)} collective-permute-done((bf16[128,1024]{1,0:T(8,128)(2,1)S(1)}, bf16[128,1024]{1,0:T(8,128)(2,1)S(1)}, u32[]{:S(2)}, u32[]{:S(2)}) %collective-permute-start) | collective-permute-done | bytes 262176 | tf_op jit(solution)/shard_map/ppermute | solution.py:324
  37.8 3.9 %collective-permute-start.12 = (f32[2,128,256]{2,1,0:T(8,128)}, f32[2,128,256]{2,1,0:T(8,128)S(1)}, u32[]{:S(2)}, u32[]{:S(2)}) collective-permute-start(f32[2,128,256]{2,1,0:T(8,128)} %get-tuple-element.51), channel_id=1, source_target_pairs={{0,0},{32,64},{64,32},{96,96},{1,1},{33,65},{65,33},{97,97},{2,2},... | collective-permute-start | bytes 786440 | tf_op jit(solution)/shard_map/ppermute | solution.py:335
  42.6 2.6 %collective-permute-start.9 = (bf16[2,128,256]{2,1,0:T(8,128)(2,1)S(1)}, bf16[2,128,256]{2,1,0:T(8,128)(2,1)S(1)}, u32[]{:S(2)}, u32[]{:S(2)}) collective-permute-start(bf16[2,128,256]{2,1,0:T(8,128)(2,1)S(1)} %get-tuple-element.28), channel_id=1, source_target_pairs={{0,24},{8,0},{16,8},{24,16},{1,25},{9,1},{17,9},{25,17},{2,26},{10... | collective-permute-start | bytes 393224 | tf_op jit(solution)/shard_map/ppermute | solution.py:293
  47.9 3.8 %attention_sums.3.refs_6_ = f32[4,128,256]{2,1,0:T(8,128)S(1)} custom-call(s32[1]{0:T(128)} %bitcast.1.refs_0_.refs_5_, bf16[2,128,4096]{2,1,0:T(8,128)(2,1)S(1)} %copy-done.3, bf16[2,128,512]{2,1,0:T(8,128)(2,1)S(1)} %copy-done.9, bf16[2,128,4096]{2,1,0:T(8,128)(2,1)S(1)} %copy-done.5, f32[2,128,256]{2,1,0:T(8,128)S(1)} %get-tuple-element.27.refs_2_.refs_4_.refs_0_), custom_call_target="tpu_custom_call" | custom-call | flops 2147483648 | bytes 1024 | tf_op jit(solution)/shard_map/attention_sums/pallas_call | solution.py:91
  51.8 3.1 %collective-permute-done.11.refs_3_ = bf16[2,128,256]{2,1,0:T(8,128)(2,1)S(1)} collective-permute-done((bf16[2,128,256]{2,1,0:T(8,128)(2,1)S(1)}, bf16[2,128,256]{2,1,0:T(8,128)(2,1)S(1)}, u32[]{:S(2)}, u32[]{:S(2)}) %collective-permute-start.11) | collective-permute-done | bytes 131104 | tf_op jit(solution)/shard_map/ppermute | solution.py:293
  57.9 6.2 %collective-permute-done.14.refs_9_ = bf16[2,128,256]{2,1,0:T(8,128)(2,1)S(1)} collective-permute-done((bf16[2,128,256]{2,1,0:T(8,128)(2,1)S(1)}, bf16[2,128,256]{2,1,0:T(8,128)(2,1)S(1)}, u32[]{:S(2)}, u32[]{:S(2)}) %collective-permute-start.14) | collective-permute-done | bytes 131104 | tf_op jit(solution)/shard_map/ppermute | solution.py:293
  65.8 6.4 %all-to-all-start.1 = ((bf16[8,2,64,256]{3,2,1,0:T(8,128)(2,1)}), bf16[8,2,64,256]{3,2,1,0:T(8,128)(2,1)S(1)}, u32[]{:S(2)}, u32[]{:S(2)}) async-start(bf16[8,2,64,256]{3,2,1,0:T(8,128)(2,1)} %partial_gradient.2.refs_2_), calls=%async_computation.1 | async-start | bytes 1048576 | tf_op jit(solution)/shard_map/all_to_all | solution.py:375
  72.2 3.9 %collective-permute-start.8 = (bf16[128,1024]{1,0:T(8,128)(2,1)S(1)}, bf16[128,1024]{1,0:T(8,128)(2,1)S(1)}, u32[]{:S(2)}, u32[]{:S(2)}) collective-permute-start(bf16[128,1024]{1,0:T(8,128)(2,1)S(1)} %slabs.4.refs_7_), channel_id=1, source_target_pairs={{0,0},{8,8},{16,16},{24,24},{32,64},{40,72},{48,80},{56,88},{64,32... | collective-permute-start | bytes 786440 | tf_op jit(solution)/shard_map/ppermute | solution.py:324
  80.0 6.4 %collective-permute-done.24 = f32[64,256]{1,0:T(8,128)S(1)} collective-permute-done((f32[64,256]{1,0:T(8,128)S(1)}, f32[64,256]{1,0:T(8,128)S(1)}, u32[]{:S(2)}, u32[]{:S(2)}) %collective-permute-start.24) | collective-permute-done | bytes 65568 | tf_op jit(solution)/shard_map/ppermute | solution.py:298
  89.7 5.3 %all-to-all-start.2 = ((bf16[8,2,64,256]{3,2,1,0:T(8,128)(2,1)}), bf16[8,2,64,256]{3,2,1,0:T(8,128)(2,1)S(1)}, u32[]{:S(2)}, u32[]{:S(2)}) async-start(bf16[8,2,64,256]{3,2,1,0:T(8,128)(2,1)} %get-tuple-element.34), calls=%async_computation.2 | async-start | bytes 1048576 | tf_op jit(solution)/shard_map/all_to_all | solution.py:382
  98.3 4.0 %collective-permute-start.18 = (bf16[128,1024]{1,0:T(8,128)(2,1)S(1)}, bf16[128,1024]{1,0:T(8,128)(2,1)S(1)}, u32[]{:S(2)}, u32[]{:S(2)}) collective-permute-start(bf16[128,1024]{1,0:T(8,128)(2,1)S(1)} %get-tuple-element.32), channel_id=1, source_target_pairs={{0,16},{8,24},{16,0},{24,8},{32,80},{40,88},{48,64},{56,72},{64,48... | collective-permute-start | bytes 786440 | tf_op jit(solution)/shard_map/ppermute | solution.py:324
  103.2 4.5 %collective-permute-done.17.refs_1_ = bf16[128,1024]{1,0:T(8,128)(2,1)S(1)} collective-permute-done((bf16[128,1024]{1,0:T(8,128)(2,1)S(1)}, bf16[128,1024]{1,0:T(8,128)(2,1)S(1)}, u32[]{:S(2)}, u32[]{:S(2)}) %collective-permute-start.17) | collective-permute-done | bytes 262176 | tf_op jit(solution)/shard_map/ppermute | solution.py:324
  109.3 5.6 %collective-permute-done.18.refs_2_ = bf16[128,1024]{1,0:T(8,128)(2,1)S(1)} collective-permute-done((bf16[128,1024]{1,0:T(8,128)(2,1)S(1)}, bf16[128,1024]{1,0:T(8,128)(2,1)S(1)}, u32[]{:S(2)}, u32[]{:S(2)}) %collective-permute-start.18) | collective-permute-done | bytes 262176 | tf_op jit(solution)/shard_map/ppermute | solution.py:324
  119.4 3.2 %collective-permute-done.27.refs_1_ = bf16[2,128,256]{2,1,0:T(8,128)(2,1)S(1)} collective-permute-done((bf16[2,128,256]{2,1,0:T(8,128)(2,1)S(1)}, bf16[2,128,256]{2,1,0:T(8,128)(2,1)S(1)}, u32[]{:S(2)}, u32[]{:S(2)}) %collective-permute-start.27) | collective-permute-done | bytes 131104 | tf_op jit(solution)/shard_map/ppermute | solution.py:293
  124.8 3.2 %collective-permute-done.29.refs_3_ = bf16[2,128,256]{2,1,0:T(8,128)(2,1)S(1)} collective-permute-done((bf16[2,128,256]{2,1,0:T(8,128)(2,1)S(1)}, bf16[2,128,256]{2,1,0:T(8,128)(2,1)S(1)}, u32[]{:S(2)}, u32[]{:S(2)}) %collective-permute-start.29) | collective-permute-done | bytes 131104 | tf_op jit(solution)/shard_map/ppermute | solution.py:293
  131.1 6.1 %collective-permute-done.30.refs_9_ = bf16[2,128,256]{2,1,0:T(8,128)(2,1)S(1)} collective-permute-done((bf16[2,128,256]{2,1,0:T(8,128)(2,1)S(1)}, bf16[2,128,256]{2,1,0:T(8,128)(2,1)S(1)}, u32[]{:S(2)}, u32[]{:S(2)}) %collective-permute-start.30) | collective-permute-done | bytes 131104 | tf_op jit(solution)/shard_map/ppermute | solution.py:293
  137.9 21.4 %all_to_all.20.refs_0_ = bf16[8,2,64,256]{3,2,1,0:T(8,128)(2,1)S(1)} all-to-all(bf16[8,2,64,256]{3,2,1,0:T(8,128)(2,1)S(1)} %partial_gradient.3), channel_id=1, replica_groups=mesh['yh'=2,'c'=2,'y'=2,'x'=4,'z'=8] {'z'}, dimensions={0} | all-to-all | bytes 1048576 | tf_op jit(solution)/shard_map/all_to_all | solution.py:375
  159.5 2.7 %collective-permute-start.34 = (f32[64,256]{1,0:T(8,128)S(1)}, f32[64,256]{1,0:T(8,128)S(1)}, u32[]{:S(2)}, u32[]{:S(2)}) collective-permute-start(f32[64,256]{1,0:T(8,128)S(1)} %get-tuple-element.42), channel_id=1, source_target_pairs={{0,128},{32,160},{128,0},{160,32},{1,129},{33,161},{129,1},{161,33... | collective-permute-start | bytes 196616 | tf_op jit(solution)/shard_map/ppermute | solution.py:298
  164.2 2.3 %collective-permute-done.35 = f32[64,256]{1,0:T(8,128)S(1)} collective-permute-done((f32[64,256]{1,0:T(8,128)S(1)}, f32[64,256]{1,0:T(8,128)S(1)}, u32[]{:S(2)}, u32[]{:S(2)}) %collective-permute-start.35) | collective-permute-done | bytes 65568 | tf_op jit(solution)/shard_map/ppermute | solution.py:298
  166.6 5.3 %collective-permute-start.36 = (f32[64,256]{1,0:T(8,128)S(1)}, f32[64,256]{1,0:T(8,128)S(1)}, u32[]{:S(2)}, u32[]{:S(2)}) collective-permute-start(f32[64,256]{1,0:T(8,128)S(1)} %add_multiply_fusion), channel_id=1, source_target_pairs={{0,64},{64,0},{1,65},{65,1},{2,66},{66,2},{3,67},{67,3},{4,68},{68... | collective-permute-start | bytes 196616 | tf_op jit(solution)/shard_map/ppermute | solution.py:298
  (107 shorter events, 47.2 us)
Async XLA Ops:
  3.0 38.9 %all-to-all-start = ((bf16[16,64,256]{2,1,0:T(8,128)(2,1)}), bf16[16,64,256]{2,1,0:T(8,128)(2,1)S(1)}, u32[]{:S(2)}, u32[]{:S(2)}) async-start(bf16[16,64,256]{2,1,0:T(8,128)(2,1)} %broadcast_in_dim.2), calls=%async_computation | async-start | bytes 1048576 | tf_op jit(solution)/shard_map/all_to_all | solution.py:344
  15.2 20.3 %collective-permute-start = (bf16[128,1024]{1,0:T(8,128)(2,1)S(1)}, bf16[128,1024]{1,0:T(8,128)(2,1)S(1)}, u32[]{:S(2)}, u32[]{:S(2)}) collective-permute-start(bf16[128,1024]{1,0:T(8,128)(2,1)S(1)} %get-tuple-element.23.refs_4_), channel_id=1, source_target_pairs={{0,0},{8,8},{16,16},{24,24},{32,64},{40,72},{48,80},{56,88},{64,32... | collective-permute-start | bytes 786440 | tf_op jit(solution)/shard_map/ppermute | solution.py:324
  19.5 15.9 %collective-permute-start.1 = (bf16[128,1024]{1,0:T(8,128)(2,1)S(1)}, bf16[128,1024]{1,0:T(8,128)(2,1)S(1)}, u32[]{:S(2)}, u32[]{:S(2)}) collective-permute-start(bf16[128,1024]{1,0:T(8,128)(2,1)S(1)} %get-tuple-element.24), channel_id=1, source_target_pairs={{0,8},{8,16},{16,24},{24,0},{32,72},{40,80},{48,88},{56,64},{64,40... | collective-permute-start | bytes 786440 | tf_op jit(solution)/shard_map/ppermute | solution.py:324
  20.6 15.9 %collective-permute-start.2 = (bf16[128,1024]{1,0:T(8,128)(2,1)S(1)}, bf16[128,1024]{1,0:T(8,128)(2,1)S(1)}, u32[]{:S(2)}, u32[]{:S(2)}) collective-permute-start(bf16[128,1024]{1,0:T(8,128)(2,1)S(1)} %get-tuple-element.25), channel_id=1, source_target_pairs={{0,16},{8,24},{16,0},{24,8},{32,80},{40,88},{48,64},{56,72},{64,48... | collective-permute-start | bytes 786440 | tf_op jit(solution)/shard_map/ppermute | solution.py:324
  24.5 12.4 %collective-permute-start.3 = (bf16[128,1024]{1,0:T(8,128)(2,1)S(1)}, bf16[128,1024]{1,0:T(8,128)(2,1)S(1)}, u32[]{:S(2)}, u32[]{:S(2)}) collective-permute-start(bf16[128,1024]{1,0:T(8,128)(2,1)S(1)} %get-tuple-element.26), channel_id=1, source_target_pairs={{0,24},{8,0},{16,8},{24,16},{32,88},{40,64},{48,72},{56,80},{64,56... | collective-permute-start | bytes 786440 | tf_op jit(solution)/shard_map/ppermute | solution.py:324
  37.8 14.0 %collective-permute-start.12 = (f32[2,128,256]{2,1,0:T(8,128)}, f32[2,128,256]{2,1,0:T(8,128)S(1)}, u32[]{:S(2)}, u32[]{:S(2)}) collective-permute-start(f32[2,128,256]{2,1,0:T(8,128)} %get-tuple-element.51), channel_id=1, source_target_pairs={{0,0},{32,64},{64,32},{96,96},{1,1},{33,65},{65,33},{97,97},{2,2},... | collective-permute-start | bytes 786440 | tf_op jit(solution)/shard_map/ppermute | solution.py:335
  41.7 10.0 %collective-permute-start.13 = (f32[2,128,256]{2,1,0:T(8,128)}, f32[2,128,256]{2,1,0:T(8,128)S(1)}, u32[]{:S(2)}, u32[]{:S(2)}) collective-permute-start(f32[2,128,256]{2,1,0:T(8,128)} %get-tuple-element.50), channel_id=1, source_target_pairs={{0,64},{32,0},{64,96},{96,32},{1,65},{33,1},{65,97},{97,33},{2,66}... | collective-permute-start | bytes 786440 | tf_op jit(solution)/shard_map/ppermute | solution.py:336
  42.6 9.2 %collective-permute-start.9 = (bf16[2,128,256]{2,1,0:T(8,128)(2,1)S(1)}, bf16[2,128,256]{2,1,0:T(8,128)(2,1)S(1)}, u32[]{:S(2)}, u32[]{:S(2)}) collective-permute-start(bf16[2,128,256]{2,1,0:T(8,128)(2,1)S(1)} %get-tuple-element.28), channel_id=1, source_target_pairs={{0,24},{8,0},{16,8},{24,16},{1,25},{9,1},{17,9},{25,17},{2,26},{10... | collective-permute-start | bytes 393224 | tf_op jit(solution)/shard_map/ppermute | solution.py:293
  45.7 9.2 %collective-permute-start.11 = (bf16[2,128,256]{2,1,0:T(8,128)(2,1)S(1)}, bf16[2,128,256]{2,1,0:T(8,128)(2,1)S(1)}, u32[]{:S(2)}, u32[]{:S(2)}) collective-permute-start(bf16[2,128,256]{2,1,0:T(8,128)(2,1)S(1)} %get-tuple-element.30), channel_id=1, source_target_pairs={{0,8},{8,16},{16,24},{24,0},{1,9},{9,17},{17,25},{25,1},{2,10},{10... | collective-permute-start | bytes 393224 | tf_op jit(solution)/shard_map/ppermute | solution.py:293
  55.2 9.0 %collective-permute-start.14 = (bf16[2,128,256]{2,1,0:T(8,128)(2,1)S(1)}, bf16[2,128,256]{2,1,0:T(8,128)(2,1)S(1)}, u32[]{:S(2)}, u32[]{:S(2)}) collective-permute-start(bf16[2,128,256]{2,1,0:T(8,128)(2,1)S(1)} %value_gradient.2.refs_8_), channel_id=1, source_target_pairs={{0,8},{8,16},{16,24},{24,0},{1,9},{9,17},{17,25},{25,1},{2,10},{10... | collective-permute-start | bytes 393224 | tf_op jit(solution)/shard_map/ppermute | solution.py:293
  55.3 8.9 %collective-permute-start.15 = (bf16[2,128,256]{2,1,0:T(8,128)(2,1)S(1)}, bf16[2,128,256]{2,1,0:T(8,128)(2,1)S(1)}, u32[]{:S(2)}, u32[]{:S(2)}) collective-permute-start(bf16[2,128,256]{2,1,0:T(8,128)(2,1)S(1)} %value_gradient.2.refs_8_), channel_id=1, source_target_pairs={{0,16},{8,24},{16,0},{24,8},{1,17},{9,25},{17,1},{25,9},{2,18},{10... | collective-permute-start | bytes 393224 | tf_op jit(solution)/shard_map/ppermute | solution.py:293
  55.7 8.5 %collective-permute-start.16 = (bf16[2,128,256]{2,1,0:T(8,128)(2,1)S(1)}, bf16[2,128,256]{2,1,0:T(8,128)(2,1)S(1)}, u32[]{:S(2)}, u32[]{:S(2)}) collective-permute-start(bf16[2,128,256]{2,1,0:T(8,128)(2,1)S(1)} %value_gradient.2.refs_8_), channel_id=1, source_target_pairs={{0,24},{8,0},{16,8},{24,16},{1,25},{9,1},{17,9},{25,17},{2,26},{10... | collective-permute-start | bytes 393224 | tf_op jit(solution)/shard_map/ppermute | solution.py:293
  65.8 22.2 %all-to-all-start.1 = ((bf16[8,2,64,256]{3,2,1,0:T(8,128)(2,1)}), bf16[8,2,64,256]{3,2,1,0:T(8,128)(2,1)S(1)}, u32[]{:S(2)}, u32[]{:S(2)}) async-start(bf16[8,2,64,256]{3,2,1,0:T(8,128)(2,1)} %partial_gradient.2.refs_2_), calls=%async_computation.1 | async-start | bytes 1048576 | tf_op jit(solution)/shard_map/all_to_all | solution.py:375
  72.2 14.2 %collective-permute-start.8 = (bf16[128,1024]{1,0:T(8,128)(2,1)S(1)}, bf16[128,1024]{1,0:T(8,128)(2,1)S(1)}, u32[]{:S(2)}, u32[]{:S(2)}) collective-permute-start(bf16[128,1024]{1,0:T(8,128)(2,1)S(1)} %slabs.4.refs_7_), channel_id=1, source_target_pairs={{0,0},{8,8},{16,16},{24,24},{32,64},{40,72},{48,80},{56,88},{64,32... | collective-permute-start | bytes 786440 | tf_op jit(solution)/shard_map/ppermute | solution.py:324
  76.1 10.3 %collective-permute-start.25 = (f32[2,128,256]{2,1,0:T(8,128)S(1)}, f32[2,128,256]{2,1,0:T(8,128)S(1)}, u32[]{:S(2)}, u32[]{:S(2)}) collective-permute-start(f32[2,128,256]{2,1,0:T(8,128)S(1)} %get-tuple-element.49), channel_id=1, source_target_pairs={{0,0},{32,64},{64,32},{96,96},{1,1},{33,65},{65,33},{97,97},{2,2},... | collective-permute-start | bytes 786440 | tf_op jit(solution)/shard_map/ppermute | solution.py:335
  78.0 8.4 %collective-permute-start.26 = (f32[2,128,256]{2,1,0:T(8,128)S(1)}, f32[2,128,256]{2,1,0:T(8,128)S(1)}, u32[]{:S(2)}, u32[]{:S(2)}) collective-permute-start(f32[2,128,256]{2,1,0:T(8,128)S(1)} %get-tuple-element.48), channel_id=1, source_target_pairs={{0,64},{32,0},{64,96},{96,32},{1,65},{33,1},{65,97},{97,33},{2,66}... | collective-permute-start | bytes 786440 | tf_op jit(solution)/shard_map/ppermute | solution.py:336
  89.7 27.1 %all-to-all-start.2 = ((bf16[8,2,64,256]{3,2,1,0:T(8,128)(2,1)}), bf16[8,2,64,256]{3,2,1,0:T(8,128)(2,1)S(1)}, u32[]{:S(2)}, u32[]{:S(2)}) async-start(bf16[8,2,64,256]{3,2,1,0:T(8,128)(2,1)} %get-tuple-element.34), calls=%async_computation.2 | async-start | bytes 1048576 | tf_op jit(solution)/shard_map/all_to_all | solution.py:382
  96.8 10.9 %collective-permute-start.17 = (bf16[128,1024]{1,0:T(8,128)(2,1)S(1)}, bf16[128,1024]{1,0:T(8,128)(2,1)S(1)}, u32[]{:S(2)}, u32[]{:S(2)}) collective-permute-start(bf16[128,1024]{1,0:T(8,128)(2,1)S(1)} %get-tuple-element.31), channel_id=1, source_target_pairs={{0,8},{8,16},{16,24},{24,0},{32,72},{40,80},{48,88},{56,64},{64,40... | collective-permute-start | bytes 786440 | tf_op jit(solution)/shard_map/ppermute | solution.py:324
  98.3 16.6 %collective-permute-start.18 = (bf16[128,1024]{1,0:T(8,128)(2,1)S(1)}, bf16[128,1024]{1,0:T(8,128)(2,1)S(1)}, u32[]{:S(2)}, u32[]{:S(2)}) collective-permute-start(bf16[128,1024]{1,0:T(8,128)(2,1)S(1)} %get-tuple-element.32), channel_id=1, source_target_pairs={{0,16},{8,24},{16,0},{24,8},{32,80},{40,88},{48,64},{56,72},{64,48... | collective-permute-start | bytes 786440 | tf_op jit(solution)/shard_map/ppermute | solution.py:324
  102.3 12.7 %collective-permute-start.19 = (bf16[128,1024]{1,0:T(8,128)(2,1)S(1)}, bf16[128,1024]{1,0:T(8,128)(2,1)S(1)}, u32[]{:S(2)}, u32[]{:S(2)}) collective-permute-start(bf16[128,1024]{1,0:T(8,128)(2,1)S(1)} %get-tuple-element.33), channel_id=1, source_target_pairs={{0,24},{8,0},{16,8},{24,16},{32,88},{40,64},{48,72},{56,80},{64,56... | collective-permute-start | bytes 786440 | tf_op jit(solution)/shard_map/ppermute | solution.py:324
  102.3 13.1 %collective-permute-start.20 = (bf16[128,1024]{1,0:T(8,128)(2,1)S(1)}, bf16[128,1024]{1,0:T(8,128)(2,1)S(1)}, u32[]{:S(2)}, u32[]{:S(2)}) collective-permute-start(bf16[128,1024]{1,0:T(8,128)(2,1)S(1)} %collective-permute-done.8.refs_4_.refs_0_), channel_id=1, source_target_pairs={{0,64},{64,0},{1,65},{65,1},{2,66},{66,2},{3,67},{67,3},{4,68},{68... | collective-permute-start | bytes 786440 | tf_op jit(solution)/shard_map/ppermute | solution.py:298
  118.7 9.3 %collective-permute-start.29 = (bf16[2,128,256]{2,1,0:T(8,128)(2,1)S(1)}, bf16[2,128,256]{2,1,0:T(8,128)(2,1)S(1)}, u32[]{:S(2)}, u32[]{:S(2)}) collective-permute-start(bf16[2,128,256]{2,1,0:T(8,128)(2,1)S(1)} %get-tuple-element.38), channel_id=1, source_target_pairs={{0,8},{8,16},{16,24},{24,0},{1,9},{9,17},{17,25},{25,1},{2,10},{10... | collective-permute-start | bytes 393224 | tf_op jit(solution)/shard_map/ppermute | solution.py:293
  128.3 8.8 %collective-permute-start.30 = (bf16[2,128,256]{2,1,0:T(8,128)(2,1)S(1)}, bf16[2,128,256]{2,1,0:T(8,128)(2,1)S(1)}, u32[]{:S(2)}, u32[]{:S(2)}) collective-permute-start(bf16[2,128,256]{2,1,0:T(8,128)(2,1)S(1)} %value_gradient.3.refs_8_), channel_id=1, source_target_pairs={{0,8},{8,16},{16,24},{24,0},{1,9},{9,17},{17,25},{25,1},{2,10},{10... | collective-permute-start | bytes 393224 | tf_op jit(solution)/shard_map/ppermute | solution.py:293
  128.4 8.7 %collective-permute-start.31 = (bf16[2,128,256]{2,1,0:T(8,128)(2,1)S(1)}, bf16[2,128,256]{2,1,0:T(8,128)(2,1)S(1)}, u32[]{:S(2)}, u32[]{:S(2)}) collective-permute-start(bf16[2,128,256]{2,1,0:T(8,128)(2,1)S(1)} %value_gradient.3.refs_8_), channel_id=1, source_target_pairs={{0,16},{8,24},{16,0},{24,8},{1,17},{9,25},{17,1},{25,9},{2,18},{10... | collective-permute-start | bytes 393224 | tf_op jit(solution)/shard_map/ppermute | solution.py:293
  (29 other events, 268.6 us)
